TPU v7x, 32 devices: a whole 2x2x4 slice. The times are simulated.
32 devices in a mesh: grp: 8 (over y, x, core), seq: 4 (over z).
Axes of the slice: x: 2, y: 2, z: 4, core: 2. Of those that a mesh axis runs over, the one named last changes fastest.
Arguments:
- frames: bfloat16 [8, 1500, 512], P('grp', 'seq'), may hold values from -6 to 6
- input_ids: int32 [8, 448], P('grp'), may hold values from 0 to 51879
- target_ids: int32 [8, 448], P('grp'), may hold values from 0 to 51879
- lengths: int32 [8], replicated, may hold values from 56 to 448, as said below
- present: int32 [8], replicated, may hold values from 0 to 1, as said below
- step_count: int32 [1], replicated, may hold values from 1 to 20
- enc_params: float32 [3392000], P(('grp', 'seq'))
- enc_moment: float32 [3392000], P(('grp', 'seq')), may hold values from -0.00012207031 to 0.00012207031
- enc_second: float32 [3392000], P(('grp', 'seq')), may hold values from 1e-11 to 1e-10
- dec_params: float32 [4194304], P(('grp', 'seq'))
- dec_moment: float32 [4194304], P(('grp', 'seq')), may hold values from -0.00012207031 to 0.00012207031
- dec_second: float32 [4194304], P(('grp', 'seq')), may hold values from 1e-11 to 1e-10
- table_params: float32 [512, 51880], P('grp', 'seq'), may hold values from -0.5 to 0.5
- table_moment: float32 [512, 51880], P('grp', 'seq'), may hold values from -0.00012207031 to 0.00012207031
- table_second: float32 [512, 51880], P('grp', 'seq'), may hold values from 1e-11 to 1e-10
Outputs:
- mean_loss: float32 [], replicated
- grad_norm: float32 [], replicated
- new_enc_params: float32 [3392000], P(('grp', 'seq'))
- new_enc_moment: float32 [3392000], P(('grp', 'seq'))
- new_enc_second: float32 [3392000], P(('grp', 'seq'))
- new_dec_params: float32 [4194304], P(('grp', 'seq'))
- new_dec_moment: float32 [4194304], P(('grp', 'seq'))
- new_dec_second: float32 [4194304], P(('grp', 'seq'))
- new_table_params: float32 [512, 51880], P('grp', 'seq')
- new_table_moment: float32 [512, 51880], P('grp', 'seq')
- new_table_second: float32 [512, 51880], P('grp', 'seq')
Inputs may be any that keep to these rules, and one draw needn't show every extreme that they name: `lengths`: some clip slot has length exactly 448. `present`: at least one slot holds a clip.
All inputs are finite; a program needn't handle non-finite values.
Results may differ from a plain program's by a relative error of at most 0.00275.
The roundings to bfloat16 on the way count: a program that leaves them out, or rounds other values in their place, can miss the bound.
Values may be sent and summed in bfloat16 or wider, within the bound.
No kernel may reach another device: no remote copies, remote signals or barrier semaphores. Data moves between devices by JAX's collectives and lax.ppermute only.
A program may use at most 320 MiB of HBM per device.

v0:
```python
from functools import partial
import math

import jax
import jax.numpy as jnp
from jax import lax
from jax.experimental import pallas as pl
from jax.experimental.pallas import tpu as pltpu
from jax.sharding import PartitionSpec as P


D = 512
HEADS = 8
F = 2048
LEN = 448
HEAD = D // HEADS
LANES = 128


beta_one = 0.9
beta_two = 0.999
rate = 0.01
decay = 0.1
adam_eps = 1e-08
clip_limit = 1.0
norm_eps = 1e-05
masked_score = -1e30

bf16 = jnp.bfloat16
f32 = jnp.float32


def layer_norm(values, norm_gain, norm_shift):
    center = values - jnp.mean(values, axis=-1, keepdims=True)
    spread = jnp.mean(center * center, axis=-1, keepdims=True)
    return center * lax.rsqrt(spread + norm_eps) * norm_gain + norm_shift


def norm_back(grad_out, values, norm_gain, norm_shift):
    _, pullback = jax.vjp(layer_norm, values, norm_gain, norm_shift)
    return pullback(grad_out)


def enc_layout():
    return [(D, 3 * D), (D, D), (D, F), (F, D), (LEN, D), (7, D), (7, D), (11, D), (2, F)]


def dec_layout():
    return [(D, 3 * D), (D, D), (D, D), (D, 2 * D), (D, D), (D, F), (F, D)]


def split_flat(flat_vec, layout):
    pieces = []
    offset = 0
    for matrix_dims in layout:
        amount = matrix_dims[0] * matrix_dims[1]
        pieces.append(flat_vec[offset : offset + amount].reshape(matrix_dims))
        offset += amount
    return pieces


def times(left_side, right_side):
    return jnp.dot(left_side, right_side, preferred_element_type=f32)


def times_back(left_side, right_side):
    return lax.dot_general(
        left_side, right_side, (((1,), (1,)), ((), ())), preferred_element_type=f32
    )


def over_rows(left_side, right_side):
    return lax.dot_general(
        left_side, right_side, (((0,), (0,)), ((), ())), preferred_element_type=f32
    )


def column_sum(values):
    return jnp.sum(values.astype(f32), axis=0)


def swap(value, axis, mask):
    count = lax.axis_size(axis)
    return lax.ppermute(value, axis, [(i, i ^ mask) for i in range(count)])


def reorder(items, rank):
    items = list(items)
    bit = 1
    while bit < len(items):
        odd = (rank & bit) != 0
        items = [jnp.where(odd, items[k ^ bit], items[k]) for k in range(len(items))]
        bit *= 2
    return items


def tree_join(items, join):
    items = list(items)
    while len(items) > 1:
        items = [join(items[k], items[k + 1]) for k in range(0, len(items), 2)]
    return items[0]


def pair_join(value, axis, join):
    for bit in bits_of(axis):
        value = join(value, swap(value, axis, bit))
    return value


def all_join(value, axis, join):
    count = lax.axis_size(axis)
    return tree_join([value] + [swap(value, axis, k) for k in range(1, count)], join)


def gather_near(value, axis):
    return [value] + [swap(value, axis, k) for k in range(1, lax.axis_size(axis))]


def trade_near(items, axis):
    return [items[0]] + [swap(items[k], axis, k) for k in range(1, len(items))]


def bits_of(axis):
    count = lax.axis_size(axis)
    found = []
    bit = 1
    while bit < count:
        found.append(bit)
        bit *= 2
    return found


def group_orders():
    far = bits_of("grp")[1:]
    return far, far[::-1]


def grow(slots, bit):
    held = sorted(slots)
    sent = jnp.stack([slots[k] for k in held])
    came = swap(sent, "grp", bit)
    for place, k in enumerate(held):
        slots[k ^ bit] = came[place]
    return slots


def gather_group(value):
    half = value.shape[0] // 2
    parts = [value[:half], value[half:]]
    results = []
    for part, order in zip(parts, group_orders()):
        slots = {0: part}
        for bit in order + [1]:
            slots = grow(slots, bit)
        results.append(slots)
    count = lax.axis_size("grp")
    return jnp.stack([jnp.concatenate([r[k] for r in results]) for k in range(count)])


def reduce_group(slots, wire, hold=f32):
    count = lax.axis_size("grp")
    sent = jnp.stack([slots[k] for k in range(count) if k & 1]).astype(wire)
    came = swap(sent, "grp", 1)
    held = {k: slots[k].astype(hold) + came[k // 2].astype(hold) for k in range(0, count, 2)}
    half = slots[0].shape[0] // 2
    results = []
    for low, order in zip((0, half), group_orders()):
        part = {k: v[low : low + half] for k, v in held.items()}
        for bit in order:
            gone = [k for k in sorted(part) if k & bit]
            came = swap(jnp.stack([part[k] for k in gone]).astype(wire), "grp", bit)
            part = {
                k: v + came[gone.index(k ^ bit)].astype(hold)
                for k, v in part.items()
                if not k & bit
            }
        results.append(part[0])
    return jnp.concatenate(results)


def gather_near_lines(block):
    half = block.shape[0] // 2
    near = gather_near(block, "seq")
    return [jnp.stack([piece[low : low + half] for piece in near])[None] for low in (0, half)]


def gather_far_lines(parts, stage):
    return [
        jnp.concatenate([part, swap(part, "grp", order[stage])])
        for part, order in zip(parts, group_orders())
    ]


def lay_out_kernel(shapes, block, rank_ref, own_a, own_b, came_a, came_b, *refs):
    outs, (lines, wide, sems) = refs[: len(shapes)], refs[len(shapes) :]
    half = block // 2
    rank = rank_ref[0]

    def copies(index, start):
        slot = index ^ rank
        far_z = slot & 3
        mate = (slot >> 2) & 1
        far_x = (slot >> 3) & 1
        far_y = (slot >> 4) & 1
        for side, place, own_ref, came_ref in (
            (0, 2 * far_y + far_x, own_a, came_a),
            (1, 2 * far_x + far_y, own_b, came_b),
        ):
            target = lines.at[pl.ds(index * block + side * half, half), :]
            sem = sems.at[2 * index + side]
            if not start:
                pltpu.make_async_copy(own_ref.at[0, 0], target, sem).wait()
                continue

            @pl.when(mate == 0)
            def _():
                pltpu.make_async_copy(own_ref.at[place, far_z], target, sem).start()

            @pl.when(mate == 1)
            def _():
                pltpu.make_async_copy(came_ref.at[place, far_z], target, sem).start()

    lax.fori_loop(0, 32, lambda index, carry: (copies(index, True), carry)[1], 0)
    lax.fori_loop(0, 32, lambda index, carry: (copies(index, False), carry)[1], 0)
    first = 0
    for out, (height, across) in zip(outs, shapes):
        step = 64
        while height % step:
            step //= 2
        if across == 1:
            out[...] = lines[first : first + height, :]
        else:

            def unfold(index, carry, out=out, across=across, step=step, first=first):
                count = step * across
                start = pl.multiple_of(first + index * count, 16)
                wide[pl.ds(0, count), :] = lines[pl.ds(start, count), :].astype(f32)
                low = pl.multiple_of(index * step, step)
                for column in range(across):
                    out[pl.ds(low, step), column * LANES : (column + 1) * LANES] = wide[
                        pl.ds(column, step, stride=across), :
                    ].astype(bf16)
                return carry

            lax.fori_loop(0, height // step, unfold, 0)
        first += height * across


def lay_out(held, came, shapes, rank):
    block = 2 * held[0].shape[2]
    total = 8 * block * held[0].shape[1]
    vmem = pl.BlockSpec(memory_space=pltpu.VMEM)
    hbm = pl.BlockSpec(memory_space=pl.ANY)
    return pl.pallas_call(
        partial(lay_out_kernel, shapes, block),
        out_shape=[jax.ShapeDtypeStruct((h, a * LANES), bf16) for h, a in shapes],
        in_specs=[pl.BlockSpec(memory_space=pltpu.SMEM)] + [hbm] * 4,
        out_specs=[vmem] * len(shapes),
        scratch_shapes=[
            pltpu.VMEM((total, LANES), bf16),
            pltpu.VMEM((64 * 16, LANES), f32),
            pltpu.SemaphoreType.DMA((64,)),
        ],
        name="lay_out",
    )(rank.reshape(1), *held, *came)


def write_lines(buffer, left, right, total, first, step, own=None):
    tall, height = left.shape
    across = (right.shape[1] if own is None else 3 * D) // LANES
    rows = step * across
    assert first % rows == 0 and height % step == 0

    def kernel(*refs):
        left_ref, right_ref, out_ref = refs[0], refs[1], refs[-1]
        got = lax.dot_general(
            left_ref[...], right_ref[...], (((0,), (0,)), ((), ())), preferred_element_type=f32
        )
        for column in range(across):
            if own is None:
                piece = got[:, column * LANES : (column + 1) * LANES]
            else:
                per = D // LANES
                source = column // per
                piece = jnp.where(
                    refs[2][0] == column % per, got[:, source * LANES : (source + 1) * LANES], 0.0
                )
            out_ref[pl.ds(column, step, stride=across), :] = piece

    specs = [
        pl.BlockSpec((tall, step), lambda i: (0, i)),
        pl.BlockSpec(right.shape, lambda i: (0, 0)),
    ]
    args = [left, right]
    if own is not None:
        specs.append(pl.BlockSpec(memory_space=pltpu.SMEM))
        args.append(own.reshape(1))
    aliases = {}
    if buffer is not None:
        specs.append(pl.BlockSpec(memory_space=pl.ANY))
        aliases = {len(args): 0}
        args.append(buffer)
    return pl.pallas_call(
        kernel,
        grid=(height // step,),
        in_specs=specs,
        out_specs=pl.BlockSpec((rows, LANES), lambda i: (first // rows + i, 0)),
        out_shape=jax.ShapeDtypeStruct((total, LANES), f32),
        input_output_aliases=aliases,
        name="write_lines",
    )(*args)


def write_rest(buffer, matrix, rest, first):
    height = matrix.shape[0]
    across = D // LANES
    rows = height * across + rest.shape[0]

    def kernel(matrix_ref, rest_ref, buffer_ref, out_ref):
        for column in range(across):
            out_ref[pl.ds(column, height, stride=across), :] = matrix_ref[
                :, column * LANES : (column + 1) * LANES
            ]
        out_ref[height * across :, :] = rest_ref[...]

    return pl.pallas_call(
        kernel,
        grid=(1,),
        in_specs=[
            pl.BlockSpec(matrix.shape, lambda i: (0, 0)),
            pl.BlockSpec(rest.shape, lambda i: (0, 0)),
            pl.BlockSpec(memory_space=pl.ANY),
        ],
        out_specs=pl.BlockSpec((rows, LANES), lambda i: (first // rows, 0)),
        out_shape=jax.ShapeDtypeStruct(buffer.shape, f32),
        input_output_aliases={2: 0},
        name="write_rest",
    )(matrix, rest, buffer)


def reduce_blocks(blocks, pick):
    group_rank = lax.axis_index("grp")
    rest = blocks.shape[2:]
    blocks = blocks.reshape((4, 2) + blocks.shape[1:])
    mine = group_rank & 1

    def entry(core):
        zero = jnp.int32(0)
        start = (zero, core, pick) + (zero,) * len(rest)
        return lax.dynamic_slice(blocks, start, (4, 1, 1) + rest).reshape((2, 2) + rest)

    def step(value, place, bit):
        mine = (group_rank & bit) // bit
        sent = lax.dynamic_slice_in_dim(value, 1 - mine, 1, place)
        kept = lax.dynamic_slice_in_dim(value, mine, 1, place)
        return kept + swap(sent, "grp", bit)

    blocks = entry(mine) + swap(entry(1 - mine), "grp", 1)
    half = rest[-2] // 2
    results = []
    for low, order in zip((0, half), group_orders()):
        part = lax.slice_in_dim(blocks, low, low + half, axis=blocks.ndim - 2)
        for bit in order:
            part = step(part, 0 if bit == 4 else 1, bit)
        results.append(part.reshape(rest[:-2] + (half, LANES)))
    return jnp.concatenate(results, axis=-2)


def scatter_near(items, axis, wire):
    came = [swap(items[k].astype(wire), axis, k).astype(f32) for k in range(1, len(items))]
    return tree_join([items[0].astype(f32)] + came, jnp.add)


def head_scores(query_ref, key_ref, bias_ref, head, causal):
    query = query_ref[...]
    lane = lax.broadcasted_iota(jnp.int32, query.shape, 1)
    query = jnp.where(lane // HEAD == head, query * jnp.bfloat16(HEAD ** (-0.5)), jnp.bfloat16(0))
    scores = times_back(key_ref[...], query)
    if causal:
        key_at = lax.broadcasted_iota(jnp.int32, scores.shape, 0)
        query_at = lax.broadcasted_iota(jnp.int32, scores.shape, 1)
        return query, jnp.where(query_at >= key_at, scores, masked_score)
    return query, scores + bias_ref[...]


def head_rows(parts):
    row = lax.broadcasted_iota(jnp.int32, parts[0].shape, 0)
    joined = parts[-1]
    for head in range(len(parts) - 2, -1, -1):
        joined = jnp.where(row < (head + 1) * HEAD, parts[head], joined)
    return joined.T


def attend_forward_kernel(causal, query_ref, key_ref, value_ref, bias_ref, out_ref, total_ref):
    parts = []
    for head in range(query_ref.shape[1] // HEAD):
        _, scores = head_scores(query_ref, key_ref, bias_ref, head, causal)
        highest = jnp.max(scores, axis=0, keepdims=True)
        weights = jnp.exp(scores - highest)
        total = jnp.sum(weights, axis=0, keepdims=True)
        weights = (weights * (1.0 / total)).astype(bf16)
        parts.append(over_rows(value_ref[...], weights))
        total_ref[head : head + 1, :] = highest + jnp.log(total)
    out_ref[...] = head_rows(parts).astype(bf16)


def query_tile(rows):
    return 256 if rows % 256 == 0 else rows


def attend_forward(query, keys, values, bias, causal=False):
    rows, wide = query.shape
    tile = query_tile(rows)
    whole = pl.BlockSpec(keys.shape, lambda i: (0, 0))
    return pl.pallas_call(
        partial(attend_forward_kernel, causal),
        grid=(rows // tile,),
        in_specs=[
            pl.BlockSpec((tile, wide), lambda i: (i, 0)),
            whole,
            whole,
            pl.BlockSpec(bias.shape, lambda i: (0, 0)),
        ],
        out_specs=[
            pl.BlockSpec((tile, wide), lambda i: (i, 0)),
            pl.BlockSpec((wide // HEAD, tile), lambda i: (0, i)),
        ],
        out_shape=[
            jax.ShapeDtypeStruct((rows, wide), bf16),
            jax.ShapeDtypeStruct((wide // HEAD, rows), f32),
        ],
        name="attend_forward",
    )(query, keys, values, bias)


def attend_backward_kernel(
    causal,
    grad_ref,
    query_ref,
    key_ref,
    value_ref,
    total_ref,
    bias_ref,
    grad_query_ref,
    grad_key_ref,
    grad_value_ref,
    key_sum,
    value_sum,
):
    @pl.when(pl.program_id(0) == 0)
    def _():
        key_sum[...] = jnp.zeros_like(key_sum)
        value_sum[...] = jnp.zeros_like(value_sum)

    grad = grad_ref[...]
    lane = lax.broadcasted_iota(jnp.int32, grad.shape, 1)
    parts = []
    for head in range(grad.shape[1] // HEAD):
        query, scores = head_scores(query_ref, key_ref, bias_ref, head, causal)
        weights = jnp.exp(scores - total_ref[head : head + 1, :])
        grad_head = jnp.where(lane // HEAD == head, grad, jnp.bfloat16(0))
        grad_weights = times_back(value_ref[...], grad_head)
        inner = jnp.sum(weights * grad_weights, axis=0, keepdims=True)
        grad_scores = (weights * (grad_weights - inner)).astype(bf16)
        value_sum[...] += times(weights.astype(bf16), grad_head)
        key_sum[...] += times(grad_scores, query)
        parts.append(over_rows(key_ref[...], grad_scores))
    grad_query_ref[...] = (head_rows(parts) * HEAD ** (-0.5)).astype(bf16)

    @pl.when(pl.program_id(0) == pl.num_programs(0) - 1)
    def _():
        grad_key_ref[...] = key_sum[...].astype(bf16)
        grad_value_ref[...] = value_sum[...].astype(bf16)


def attend_backward(grad_mixed, query, keys, values, log_total, bias, causal=False):
    rows, wide = query.shape
    tile = query_tile(rows)
    some = pl.BlockSpec((tile, wide), lambda i: (i, 0))
    whole = pl.BlockSpec(keys.shape, lambda i: (0, 0))
    return pl.pallas_call(
        partial(attend_backward_kernel, causal),
        grid=(rows // tile,),
        in_specs=[
            some,
            some,
            whole,
            whole,
            pl.BlockSpec((wide // HEAD, tile), lambda i: (0, i)),
            pl.BlockSpec(bias.shape, lambda i: (0, 0)),
        ],
        out_specs=[some, whole, whole],
        out_shape=[
            jax.ShapeDtypeStruct((rows, wide), bf16),
            jax.ShapeDtypeStruct(keys.shape, bf16),
            jax.ShapeDtypeStruct(keys.shape, bf16),
        ],
        scratch_shapes=[pltpu.VMEM(keys.shape, f32), pltpu.VMEM(keys.shape, f32)],
        name="attend_backward",
    )(grad_mixed, query, keys, values, log_total, bias)


def stand_up(rows):
    blank = jnp.zeros((LANES - rows.shape[0], rows.shape[1]), rows.dtype)
    return jnp.concatenate([rows, blank]).T


def loss_forward_kernel(last, rank_ref, here_ref, states_ref, table_ref, target_ref, out_ref):
    target = stand_up(jnp.broadcast_to(target_ref[0].astype(f32), (8, target_ref.shape[2])))
    target = target[:, 0:1].astype(jnp.int32)

    def work(columns, short):
        logits = times(states_ref[0], table_ref[:, :columns])
        column = lax.broadcasted_iota(jnp.int32, logits.shape, 1)
        if short:
            logits = jnp.where(column < here_ref[0], logits, masked_score)
        highest = jnp.max(logits, axis=1, keepdims=True)
        total = jnp.sum(jnp.exp(logits - highest), axis=1, keepdims=True)
        picked = jnp.sum(jnp.where(column == target, logits, 0.0), axis=1, keepdims=True)
        lane = lax.broadcasted_iota(jnp.int32, (logits.shape[0], LANES), 1)
        packed = jnp.where(lane == 0, highest, jnp.where(lane == 1, total, picked))
        out_ref[0] = packed.T[:8]

    width = table_ref.shape[1]

    @pl.when(here_ref[0] == width)
    def _():
        work(width, False)

    @pl.when(here_ref[0] != width)
    def _():
        work(round_up(last, LANES), True)


def loss_forward(states, table, targets, here, rank, last):
    count, tile, deep = states.shape
    return pl.pallas_call(
        partial(loss_forward_kernel, last),
        grid_spec=pltpu.PrefetchScalarGridSpec(
            num_scalar_prefetch=2,
            grid=(count,),
            in_specs=[
                pl.BlockSpec((1, tile, deep), lambda i, rank, here: (i, 0, 0)),
                pl.BlockSpec(table.shape, lambda i, rank, here: (0, 0)),
                pl.BlockSpec((1, 1, tile), lambda i, rank, here: (i, 0, 0)),
            ],
            out_specs=pl.BlockSpec((1, 8, tile), lambda i, rank, here: (i ^ rank[0], 0, 0)),
        ),
        out_shape=jax.ShapeDtypeStruct((count, 8, tile), f32),
        name="loss_forward",
    )(rank.reshape(1), here.reshape(1), states, table, targets)


def join_stats_kernel(*refs):
    parts, out_ref = [ref[...] for ref in refs[:-1]], refs[-1]
    while len(parts) > 1:
        pairs = []
        for first, second in zip(parts[::2], parts[1::2]):
            biggest = jnp.maximum(first[:, 0:1], second[:, 0:1])
            summed = first[:, 1:2] * jnp.exp(first[:, 0:1] - biggest) + second[:, 1:2] * jnp.exp(
                second[:, 0:1] - biggest
            )
            picked = first[:, 2:3] + second[:, 2:3]
            pairs.append(jnp.concatenate([biggest, summed, picked, first[:, 3:]], axis=1))
        parts = pairs
    out_ref[...] = parts[0]


def join_stats(parts):
    vmem = pl.BlockSpec(memory_space=pltpu.VMEM)
    return pl.pallas_call(
        join_stats_kernel,
        in_specs=[vmem] * len(parts),
        out_specs=vmem,
        out_shape=jax.ShapeDtypeStruct(parts[0].shape, f32),
        name="join_stats",
    )(*parts)


def loss_backward_kernel(
    last, rank_ref, here_ref, states_ref, table_ref, target_ref, scale_ref, grad_ref, out_ref
):
    target = stand_up(jnp.broadcast_to(target_ref[0].astype(f32), (8, target_ref.shape[2])))
    target = target[:, 0:1].astype(jnp.int32)
    scale = stand_up(scale_ref[0])

    def work(columns, short):
        logits = times(states_ref[0], table_ref[:, :columns])
        column = lax.broadcasted_iota(jnp.int32, logits.shape, 1)
        soft = jnp.exp(logits - scale[:, 0:1])
        grad = jnp.where(column == target, soft - 1.0, soft) * scale[:, 1:2]
        if short:
            grad = jnp.where(column < here_ref[0], grad, 0.0)
        grad = grad.astype(bf16)
        grad_ref[0, :, :columns] = grad
        if columns < grad_ref.shape[2]:
            grad_ref[0, :, columns:] = jnp.zeros(
                (grad.shape[0], grad_ref.shape[2] - columns), bf16
            )
        out_ref[0] = times_back(grad, table_ref[:, :columns])

    width = table_ref.shape[1]

    @pl.when(here_ref[0] == width)
    def _():
        work(width, False)

    @pl.when(here_ref[0] != width)
    def _():
        work(round_up(last, LANES), True)


def loss_backward(states, table, targets, scales, here, rank, last):
    count, tile, deep = states.shape
    width = table.shape[1]
    return pl.pallas_call(
        partial(loss_backward_kernel, last),
        grid_spec=pltpu.PrefetchScalarGridSpec(
            num_scalar_prefetch=2,
            grid=(count,),
            in_specs=[
                pl.BlockSpec((1, tile, deep), lambda i, rank, here: (i, 0, 0)),
                pl.BlockSpec(table.shape, lambda i, rank, here: (0, 0)),
                pl.BlockSpec((1, 1, tile), lambda i, rank, here: (i, 0, 0)),
                pl.BlockSpec((1, 2, tile), lambda i, rank, here: (i ^ rank[0], 0, 0)),
            ],
            out_specs=[
                pl.BlockSpec((1, tile, width), lambda i, rank, here: (i, 0, 0)),
                pl.BlockSpec((1, tile, deep), lambda i, rank, here: (i, 0, 0)),
            ],
        ),
        out_shape=[
            jax.ShapeDtypeStruct((count, tile, width), bf16),
            jax.ShapeDtypeStruct((count, tile, deep), f32),
        ],
        name="loss_backward",
    )(rank.reshape(1), here.reshape(1), states, table, targets, scales)


def own_blocks_kernel(pieces, lines, rank_ref, *refs):
    out_ref, stage = refs[-2], refs[-1]
    count = out_ref.shape[0]

    def branch(seq_rank):
        for place in range(count):
            low = (4 * place + seq_rank) * lines
            for first, left, right in pieces:
                left_ref, right_ref = refs[left], refs[right]
                across = right_ref.shape[1] // LANES
                last = first + left_ref.shape[1] * across
                if not first <= low < last:
                    continue
                top = (low - first) // across
                bottom = -(-(low + lines - first) // across)
                skip = low - first - top * across
                got = lax.dot_general(
                    left_ref[:, top:bottom],
                    right_ref[...],
                    (((0,), (0,)), ((), ())),
                    preferred_element_type=f32,
                )
                target = stage if (bottom - top) * across != lines else out_ref.at[place]
                for column in range(across):
                    target[pl.ds(column, bottom - top, stride=across), :] = got[
                        :, column * LANES : (column + 1) * LANES
                    ]
                if target is stage:
                    out_ref[place] = stage[skip : skip + lines, :]

    for seq_rank in range(4):

        @pl.when(rank_ref[0] == seq_rank)
        def _(seq_rank=seq_rank):
            branch(seq_rank)


def own_blocks(pairs, firsts, lines, count, seq_rank):
    vmem = pl.BlockSpec(memory_space=pltpu.VMEM)
    args = [value for pair in pairs for value in pair]
    pieces = [(first, 2 * k, 2 * k + 1) for k, first in enumerate(firsts)]
    return pl.pallas_call(
        partial(own_blocks_kernel, pieces, lines),
        in_specs=[pl.BlockSpec(memory_space=pltpu.SMEM)] + [vmem] * len(args),
        out_specs=vmem,
        out_shape=jax.ShapeDtypeStruct((count, lines, LANES), f32),
        scratch_shapes=[pltpu.VMEM((lines + 64, LANES), f32)],
        name="own_blocks",
    )(seq_rank.reshape(1), *args)


def mlp_forward(stream, norm_gain, norm_shift, w_up, b_up, w_down, b_down):
    normed = layer_norm(stream, norm_gain, norm_shift).astype(bf16)
    raised = times(normed, w_up) + b_up
    active = jax.nn.gelu(raised, approximate=False).astype(bf16)
    return (stream + times(active, w_down) + b_down, normed, raised, active)


def mlp_backward(grad_stream, stream, norm_gain, norm_shift, raised, w_up, w_down):
    grad_branch = grad_stream.astype(bf16)
    grad_bdown = column_sum(grad_branch)
    grad_active = times_back(grad_branch, w_down)
    _, gelu_pull = jax.vjp(partial(jax.nn.gelu, approximate=False), raised)
    grad_raised = gelu_pull(grad_active)[0].astype(bf16)
    grad_bup = column_sum(grad_raised)
    grad_normed = times_back(grad_raised, w_up)
    grad_in, grad_gain, grad_shift = norm_back(grad_normed, stream, norm_gain, norm_shift)
    return (
        grad_stream + grad_in,
        grad_branch,
        grad_raised,
        grad_bup,
        grad_bdown,
        grad_gain,
        grad_shift,
    )


def adamw(weight_now, moment, second, gradient, factor, bias_one, bias_two):
    scaled = gradient * factor
    new_moment = beta_one * moment + (1.0 - beta_one) * scaled
    new_second = beta_two * second + (1.0 - beta_two) * scaled * scaled
    step_size = (
        new_moment / bias_one / (jnp.sqrt(new_second / bias_two) + adam_eps) + decay * weight_now
    )
    return (weight_now - rate * step_size, new_moment, new_second)


def round_up(amount, unit):
    return -(-amount // unit) * unit


def on_device(*args):
    return train_step(*args)


def train_step(
    frames,
    input_ids,
    target_ids,
    lengths,
    present,
    step_count,
    enc_params,
    enc_moment,
    enc_second,
    dec_params,
    dec_moment,
    dec_second,
    table_params,
    table_moment,
    table_second,
):
    seq_size = lax.axis_size("seq")
    grp_size = lax.axis_size("grp")
    seq_rank = lax.axis_index("seq")
    group_rank = lax.axis_index("grp")
    lead = (seq_rank == 0).astype(f32)

    frame_rows = frames.shape[1]
    rows = round_up(frame_rows, 128)
    rank = group_rank * seq_size + seq_rank
    devices = grp_size * seq_size
    enc_count = enc_params.shape[0]
    enc_lines = round_up(enc_count, 64 * LANES) // LANES
    lag = enc_lines * LANES - enc_count
    enc_here = enc_params.astype(bf16)
    enc_next = lax.ppermute(
        enc_here[: lag * devices], ("grp", "seq"), [(i + 1, i) for i in range(devices - 1)]
    )
    enc_block = lax.dynamic_slice_in_dim(
        jnp.concatenate([enc_here, enc_next]), lag * rank, enc_lines * LANES
    ).reshape(enc_lines, LANES)
    dec_lines = dec_params.shape[0] // LANES
    enc_parts = gather_near_lines(enc_block)
    frame_slots = gather_near(jnp.pad(frames[0], ((0, rows - frame_rows), (0, 0))), "seq")
    dec_parts = gather_near_lines(dec_params.astype(bf16).reshape(dec_lines, LANES))
    enc_parts = gather_far_lines(enc_parts, 0)
    enc_parts = gather_far_lines(enc_parts, 1)
    enc_came = [swap(part, "grp", 1) for part in enc_parts]
    dec_parts = gather_far_lines(dec_parts, 0)
    dec_parts = gather_far_lines(dec_parts, 1)
    dec_came = [swap(part, "grp", 1) for part in dec_parts]
    vocab = table_params.shape[1]
    width = round_up(round_up(vocab, grp_size) // grp_size, 128)
    ids_here = jnp.concatenate([input_ids, target_ids])
    ids_rows = jnp.concatenate([ids_here >> 8, ids_here & 255]).astype(bf16).reshape(1, -1)
    spare = 16 * width - ids_rows.shape[1]
    ids_rows = jnp.pad(ids_rows, ((0, 0), (0, spare))).reshape(16, width)
    table_wide = jnp.concatenate(
        [
            jnp.pad(table_params.astype(bf16), ((0, 0), (0, width * grp_size - vocab))),
            jnp.tile(ids_rows, (1, grp_size)),
        ]
    )
    chans = D // grp_size
    table_came = trade_near(
        [
            lax.dynamic_slice_in_dim(table_wide, (group_rank ^ k) * width, width, 1)
            for k in range(grp_size)
        ],
        "grp",
    )
    table = jnp.concatenate(reorder([piece[:chans] for piece in table_came], group_rank))
    vocab_first = seq_rank * vocab + group_rank * width
    vocab_here = jnp.clip(vocab - group_rank * width, 0, width)
    ids_slots = jnp.stack([piece[chans:] for piece in table_came]).reshape(grp_size, -1)
    ids_slots = ids_slots[:, : 4 * LEN].astype(jnp.int32).reshape(grp_size, 2, 2, LEN)
    ids_slots = ids_slots[:, 0] * 256 + ids_slots[:, 1]

    small = (7 + 7 + 11) * D + 2 * F
    enc_qkv, enc_wout, enc_wup, enc_wdown, positions, small_lines = lay_out(
        enc_parts,
        enc_came,
        [(h, w // LANES) for h, w in enc_layout()[:5]] + [(small // LANES, 1)],
        rank,
    )
    gains, shifts, biases, up_bias = split_flat(
        small_lines.astype(f32).reshape(-1), enc_layout()[5:]
    )
    positions = positions.astype(f32)
    span = D // seq_size

    def own(matrix, parts):
        return jnp.concatenate(
            [
                lax.dynamic_slice_in_dim(matrix, part * D + seq_rank * span, span, matrix.ndim - 1)
                for part in range(parts)
            ],
            axis=-1,
        )

    def own_bias(row):
        return lax.dynamic_slice_in_dim(biases[row], seq_rank * span, span, 0)

    half_width = D // 2
    stride = math.log(10000.0) / (half_width - 1)
    inverse = jnp.exp(-stride * jnp.arange(half_width, dtype=f32))
    x_slots = []
    for k in range(seq_size):
        offset = ((seq_rank ^ k) * frame_rows).astype(f32)
        angles = (jnp.arange(rows, dtype=f32) + offset)[:, None] * inverse[None, :]
        wave = jnp.concatenate([jnp.sin(angles), jnp.cos(angles)], axis=1)
        x_slots.append(frame_slots[k].astype(f32) + wave)
    x_all = jnp.concatenate(x_slots)
    x_enc0 = x_slots[0]
    h_enc1 = layer_norm(x_all, gains[0], shifts[0]).astype(bf16)
    own_enc_qkv = own(enc_qkv, 3)
    packed = times(h_enc1, own_enc_qkv)
    q_enc = (packed[:, :span] + own_bias(0)).astype(bf16)
    k_enc = packed[:, span : 2 * span].astype(bf16)
    v_enc = (packed[:, 2 * span :] + own_bias(1)).astype(bf16)
    frame_bias = jnp.where(jnp.arange(rows * seq_size) % rows < frame_rows, 0.0, masked_score)
    frame_bias = frame_bias.astype(f32)[:, None]
    o_own, lse_enc = attend_forward(q_enc, k_enc, v_enc, frame_bias)

    def to_rows(value):
        pieces = [value[k * rows : (k + 1) * rows] for k in range(seq_size)]
        return jnp.concatenate(reorder(trade_near(pieces, "seq"), seq_rank), axis=1)

    def to_heads(value):
        pieces = reorder([value[:, k * span : (k + 1) * span] for k in range(seq_size)], seq_rank)
        return jnp.concatenate(trade_near(pieces, "seq"), axis=0)

    def two_to_heads(first, second):
        pieces = reorder(
            [
                jnp.concatenate(
                    [first[:, k * span : (k + 1) * span], second[:, k * span : (k + 1) * span]], axis=1
                )
                for k in range(seq_size)
            ],
            seq_rank,
        )
        return jnp.concatenate(trade_near(pieces, "seq"), axis=0)

    def two_to_rows(first, second):
        both = jnp.concatenate([first, second], axis=1)
        pieces = [both[k * rows : (k + 1) * rows] for k in range(seq_size)]
        pieces = reorder(trade_near(pieces, "seq"), seq_rank)
        return jnp.concatenate(
            [piece[:, :span] for piece in pieces] + [piece[:, span:] for piece in pieces], axis=1
        )

    o_enc = to_rows(o_own)
    x_enc1 = x_enc0 + times(o_enc, enc_wout) + biases[2]
    x_enc2, h_enc2, up_enc, act_enc = mlp_forward(
        x_enc1, gains[1], shifts[1], enc_wup, up_bias[0], enc_wdown, biases[3]
    )
    enc_out = layer_norm(x_enc2, gains[2], shifts[2]).astype(bf16)
    dec_qkv, dec_wout, cross_wq, cross_wkv, cross_wout, dec_wup, dec_wdown = lay_out(
        dec_parts, dec_came, [(h, w // LANES) for h, w in dec_layout()], rank
    )
    paired = times(enc_out, cross_wkv)
    k_rows = paired[:, :D].astype(bf16)
    v_rows = (paired[:, D:] + biases[8]).astype(bf16)
    pair_cross = two_to_heads(k_rows, v_rows)
    k_cross = pair_cross[:, :span]
    v_cross = pair_cross[:, span:]

    ids = ids_slots[:, 0].reshape(-1)
    columns = jnp.arange(width)[None, :]
    inside = columns < vocab_here
    id_hot = ((ids[:, None] - vocab_first == columns) & inside).astype(bf16)
    looked = times_back(id_hot, table).astype(bf16).reshape(grp_size, LEN, D)
    part_rows = LEN // seq_size

    def share_rows(value, wire):
        pieces = [value[k * part_rows : (k + 1) * part_rows] for k in range(seq_size)]
        mine = scatter_near(reorder(pieces, seq_rank), "seq", wire)
        return jnp.concatenate(reorder(gather_near(mine.astype(wire), "seq"), seq_rank))

    token_emb = reduce_group(looked, bf16, bf16)
    token_emb = share_rows(token_emb, bf16).astype(f32)

    def all_heads(value):
        return reorder(gather_near(value, "seq"), seq_rank)

    x_dec0 = token_emb + positions
    h_dec1 = layer_norm(x_dec0, gains[3], shifts[3]).astype(bf16)
    packed = times(h_dec1, own(dec_qkv, 3))
    q_dec = (packed[:, :span] + own_bias(4)).astype(bf16)
    k_dec = packed[:, span : 2 * span].astype(bf16)
    v_dec = (packed[:, 2 * span :] + own_bias(5)).astype(bf16)
    no_bias = jnp.zeros((8, 1), f32)
    o_own_dec, lse_dec = attend_forward(q_dec, k_dec, v_dec, no_bias, True)
    o_dec = jnp.concatenate(all_heads(o_own_dec), axis=1)
    x_dec1 = x_dec0 + times(o_dec, dec_wout) + biases[6]
    h_dec2 = layer_norm(x_dec1, gains[4], shifts[4]).astype(bf16)
    q_cross = (times(h_dec2, own(cross_wq, 1)) + own_bias(7)).astype(bf16)
    o_own_cross, lse_cross = attend_forward(q_cross, k_cross, v_cross, frame_bias)
    o_cross = jnp.concatenate(all_heads(o_own_cross), axis=1)
    x_dec2 = x_dec1 + times(o_cross, cross_wout) + biases[9]
    x_dec3, h_dec3, up_dec, act_dec = mlp_forward(
        x_dec2, gains[5], shifts[5], dec_wup, up_bias[1], dec_wdown, biases[10]
    )
    states = layer_norm(x_dec3, gains[6], shifts[6]).astype(bf16)

    all_states = gather_group(states)
    target_rows = ids_slots[:, 1] - vocab_first
    target_rows = jnp.where(target_rows < vocab_here, target_rows, -1)[:, None, :]
    last = vocab - (grp_size - 1) * width
    stats = loss_forward(all_states, table, target_rows, vocab_here, group_rank, last)
    for bit in bits_of("grp"):
        stats = join_stats([stats, swap(stats, "grp", bit)])
    stats = join_stats(gather_near(stats, "seq"))
    log_total = stats[:, 0] + jnp.log(stats[:, 1])
    valid = (
        (jnp.arange(LEN)[None, :] < lengths[:, None]) & (present[:, None] > 0)
    ).astype(f32)
    token_total = jnp.sum((lengths * present).astype(f32))
    row_weight = valid / token_total
    scales = jnp.stack([log_total, row_weight], axis=1)
    loss_sum = jnp.sum((log_total - stats[:, 2]) * valid)
    grad_logits, grad_states_all = loss_backward(
        all_states, table, target_rows, scales, vocab_here, group_rank, last
    )
    grad_states = share_rows(reduce_group(grad_states_all, bf16), bf16).astype(f32)

    table_main = lax.optimization_barrier(
        over_rows(all_states.reshape(-1, D), grad_logits.reshape(-1, width))
    )

    grad_x3, grad_g6, grad_s6 = norm_back(grad_states, x_dec3, gains[6], shifts[6])
    dec_at = [0]
    for height, across in dec_layout():
        dec_at.append(dec_at[-1] + height * across // LANES)
    grad_x2, grad_down_dec, grad_up_dec, grad_dec_bup, grad_b10, grad_g5, grad_s5 = mlp_backward(
        grad_x3, x_dec2, gains[5], shifts[5], up_dec, dec_wup, dec_wdown
    )
    grad_branch = grad_x2.astype(bf16)
    grad_cross_out = grad_branch
    grad_b9 = column_sum(grad_branch)
    own_cross_wout = lax.dynamic_slice_in_dim(cross_wout, seq_rank * span, span, 0)
    grad_mixed = times_back(grad_branch, own_cross_wout).astype(bf16)
    grad_qc_own, grad_kc_own, grad_vc_own = attend_backward(
        grad_mixed, q_cross, k_cross, v_cross, lse_cross, frame_bias
    )
    grad_qc = jnp.concatenate(all_heads(grad_qc_own), axis=1)
    grad_pair = two_to_rows(grad_kc_own, grad_vc_own)
    grad_b7 = column_sum(grad_qc)
    grad_in, grad_g4, grad_s4 = norm_back(
        times_back(grad_qc, cross_wq), x_dec1, gains[4], shifts[4]
    )
    grad_x1 = grad_x2 + grad_in
    grad_branch = grad_x1.astype(bf16)
    grad_self_out = grad_branch
    grad_b6 = column_sum(grad_branch)
    own_dec_wout = lax.dynamic_slice_in_dim(dec_wout, seq_rank * span, span, 0)
    grad_mixed = times_back(grad_branch, own_dec_wout).astype(bf16)
    grad_qkv_own = attend_backward(grad_mixed, q_dec, k_dec, v_dec, lse_dec, no_bias, True)
    grad_qkv_own = jnp.concatenate(grad_qkv_own, axis=1)
    grad_qkv_all = all_heads(grad_qkv_own)
    grad_packed = jnp.concatenate(
        [
            piece[:, part * span : (part + 1) * span]
            for part in range(3)
            for piece in grad_qkv_all
        ],
        axis=1,
    )
    sums = column_sum(grad_packed)
    grad_b4 = sums[:D]
    grad_b5 = sums[2 * D :]
    grad_in, grad_g3, grad_s3 = norm_back(
        times_back(grad_packed, dec_qkv), x_dec0, gains[3], shifts[3]
    )
    grad_x0 = grad_x1 + grad_in

    grad_embed_all = gather_group(grad_x0.astype(bf16)).reshape(-1, D)
    grad_table = table_main + over_rows(grad_embed_all, id_hot)
    table_back = trade_near(
        [
            lax.dynamic_slice_in_dim(grad_table, (group_rank ^ k) * chans, chans, 0)
            for k in range(grp_size)
        ],
        "grp",
    )
    table_grad = jnp.concatenate(reorder(table_back, group_rank), axis=1)
    table_grad = table_grad[:, :vocab]

    wkv_buf = write_lines(None, enc_out, grad_pair, 2 * D * D // LANES, 0, 128)
    grad_b8 = column_sum(grad_pair[:, D:])
    grad_enc2, grad_g2, grad_s2 = norm_back(
        times_back(grad_pair, cross_wkv), x_enc2, gains[2], shifts[2]
    )

    dec_mine = own_blocks(
        [
            (h_dec1, grad_packed),
            (o_dec, grad_self_out),
            (h_dec2, grad_qc),
            (o_cross, grad_cross_out),
            (h_dec3, grad_up_dec),
            (act_dec, grad_down_dec),
        ],
        [dec_at[k] for k in (0, 1, 2, 4, 5, 6)],
        dec_lines,
        grp_size,
        seq_rank,
    )
    first_block = dec_at[3] // dec_lines
    turn = first_block % seq_size
    wkv_blocks = wkv_buf.reshape(seq_size, dec_lines, LANES)
    wkv_mine = scatter_near(
        [
            lax.dynamic_index_in_dim(wkv_blocks, (seq_rank ^ k) ^ turn, 0, False)
            for k in range(seq_size)
        ],
        "seq",
        f32,
    )
    wkv_place = (first_block + (seq_rank ^ turn)) // seq_size
    dec_mine = jnp.stack(
        [jnp.where(wkv_place == k, wkv_mine, dec_mine[k]) for k in range(grp_size)]
    )
    dec_grad = reduce_blocks(dec_mine[:, None], jnp.int32(0)).reshape(-1)

    enc_at = [0]
    for height, across in enc_layout()[:5]:
        enc_at.append(enc_at[-1] + height * across // LANES)
    enc_total = enc_lines * devices
    grad_enc1, grad_down, grad_up, grad_enc_bup, grad_b3, grad_g1, grad_s1 = mlp_backward(
        grad_enc2, x_enc1, gains[1], shifts[1], up_enc, enc_wup, enc_wdown
    )
    enc_buf = write_lines(None, act_enc, grad_down, enc_total, enc_at[3], 512)
    enc_buf = write_lines(enc_buf, h_enc2, grad_up, enc_total, enc_at[2], 128)
    grad_branch = grad_enc1.astype(bf16)
    enc_buf = write_lines(enc_buf, o_enc, grad_branch, enc_total, enc_at[1], 128)
    grad_b2 = column_sum(grad_branch)
    grad_mixed = times_back(grad_branch, enc_wout).astype(bf16)
    grad_mixed = to_heads(grad_mixed)
    grad_q, grad_k, grad_v = attend_backward(grad_mixed, q_enc, k_enc, v_enc, lse_enc, frame_bias)
    grad_packed = jnp.concatenate([grad_q, grad_k, grad_v], axis=1)
    enc_buf = write_lines(enc_buf, h_enc1, grad_packed, enc_total, 0, 128, own=seq_rank)
    sums = column_sum(grad_packed)

    def placed(values):
        return lax.dynamic_update_slice(jnp.zeros((D,), f32), values, (seq_rank * span,))

    grad_b0 = placed(sums[:span])
    grad_b1 = placed(sums[2 * span :])
    _, grad_g0, grad_s0 = norm_back(
        times_back(grad_packed, own_enc_qkv), x_all, gains[0], shifts[0]
    )
    once = lead
    grad_gains = jnp.stack(
        [grad_g0, grad_g1, grad_g2, grad_g3 * once, grad_g4 * once, grad_g5 * once, grad_g6 * once]
    )
    grad_shifts = jnp.stack(
        [grad_s0, grad_s1, grad_s2, grad_s3 * once, grad_s4 * once, grad_s5 * once, grad_s6 * once]
    )
    grad_biases = jnp.stack(
        [
            grad_b0,
            grad_b1,
            grad_b2,
            grad_b3,
            grad_b4 * once,
            grad_b5 * once,
            grad_b6 * once,
            grad_b7 * once,
            grad_b8,
            grad_b9 * once,
            grad_b10 * once,
        ]
    )
    grad_up_bias = jnp.stack([grad_enc_bup, grad_dec_bup * once])
    rest = jnp.concatenate(
        [grad_gains.reshape(-1), grad_shifts.reshape(-1), grad_biases.reshape(-1), grad_up_bias.reshape(-1)]
    ).reshape(-1, LANES)
    rest = jnp.pad(rest, ((0, enc_total - enc_at[5] - rest.shape[0]), (0, 0)))
    enc_buf = write_rest(enc_buf, grad_x0 * once, rest, enc_at[4])
    pairs = enc_buf.reshape(grp_size, 2, 2, enc_lines, LANES)
    upper = seq_rank // 2
    odd = seq_rank % 2
    away = reduce_blocks(pairs, 1 - upper)
    near = reduce_blocks(lax.optimization_barrier(pairs), upper)
    parts = [
        swap(lax.dynamic_index_in_dim(away, odd, 0, False), "seq", 2),
        swap(lax.dynamic_index_in_dim(away, 1 - odd, 0, False), "seq", 3),
    ]
    parts.append(swap(lax.dynamic_index_in_dim(near, 1 - odd, 0, False), "seq", 1))
    enc_sum = lax.dynamic_index_in_dim(near, odd, 0, False) + parts[2] + (parts[0] + parts[1])
    enc_prev = lax.ppermute(
        enc_sum[enc_lines - lag * devices // LANES :].reshape(-1),
        ("grp", "seq"),
        [(i, i + 1) for i in range(devices - 1)],
    )
    enc_grad = lax.dynamic_slice_in_dim(
        jnp.concatenate([enc_prev, enc_sum.reshape(-1)]), lag * (devices - rank), enc_count
    )

    squares = (
        jnp.sum(enc_sum * enc_sum)
        + jnp.sum(dec_grad * dec_grad)
        + jnp.sum(table_grad * table_grad)
    )
    squares = all_join(pair_join(squares.reshape(1, 1), "grp", jnp.add), "seq", jnp.add)
    mean_loss = loss_sum / token_total
    grad_norm = jnp.sqrt(squares[0, 0])
    factor = jnp.minimum(1.0, clip_limit / (grad_norm + 1e-06))
    steps_done = step_count[0].astype(f32)
    bias_one = 1.0 - beta_one**steps_done
    bias_two = 1.0 - beta_two**steps_done
    enc_new = adamw(enc_params, enc_moment, enc_second, enc_grad, factor, bias_one, bias_two)
    dec_new = adamw(dec_params, dec_moment, dec_second, dec_grad, factor, bias_one, bias_two)
    table_new = adamw(
        table_params, table_moment, table_second, table_grad, factor, bias_one, bias_two
    )
    return (mean_loss, grad_norm, *enc_new, *dec_new, *table_new)


def wide_joined_2(value, axis, join):
    pieces = jax.tree.map(lambda part: lax.all_gather(part, axis), value)
    head = jax.tree.map(lambda part: part[0], pieces)
    tail = jax.tree.map(lambda part: part[1:], pieces)
    total, _ = lax.scan(lambda total, piece: (join(total, piece), None), head, tail)
    return total


def wide_sinusoid(amount, channels, offset):
    half_width = channels // 2
    stride = math.log(10000.0) / (half_width - 1)
    inverse = jnp.exp(-stride * jnp.arange(half_width, dtype=jnp.float32))
    angles = (jnp.arange(amount, dtype=jnp.float32) + offset)[:, None] * inverse[None, :]
    return jnp.concatenate([jnp.sin(angles), jnp.cos(angles)], axis=1)


def wide_times_rows(left_side, right_side):
    return lax.dot_general(
        left_side,
        right_side,
        (((left_side.ndim - 1,), (0,)), ((), ())),
        preferred_element_type=jnp.float32,
    )


def wide_times_back(left_side, right_side):
    return lax.dot_general(
        left_side,
        right_side,
        (((left_side.ndim - 1,), (1,)), ((), ())),
        preferred_element_type=jnp.float32,
    )


def wide_over_rows(left_side, right_side):
    return lax.dot_general(
        left_side, right_side, (((0, 1), (0, 1)), ((), ())), preferred_element_type=jnp.float32
    )


def wide_column_sum(values):
    return jnp.sum(values.astype(jnp.float32), axis=(0, 1))


def wide_split_heads(values):
    return values.reshape(values.shape[0], values.shape[1], HEADS, values.shape[2] // HEADS)


def wide_score_block(query, keys, first_row):
    head_size = query.shape[2] // HEADS
    scores = jnp.einsum(
        "cqhd,ckhd->chqk", wide_split_heads(query), wide_split_heads(keys), preferred_element_type=jnp.float32
    ) * head_size ** (-0.5)
    if first_row is not None:
        allowed = (first_row + jnp.arange(query.shape[1]))[:, None] >= jnp.arange(keys.shape[1])[
            None, :
        ]
        scores = jnp.where(allowed[None, None], scores, masked_score)
    return scores


def wide_attend_forward(query, keys, values, first_row):
    scores = wide_score_block(query, keys, first_row)
    highest_score = jnp.max(scores, axis=-1, keepdims=True)
    log_total = highest_score + jnp.log(
        jnp.sum(jnp.exp(scores - highest_score), axis=-1, keepdims=True)
    )
    weights = jnp.exp(scores - log_total).astype(jnp.bfloat16)
    mixed = jnp.einsum(
        "chqk,ckhd->cqhd", weights, wide_split_heads(values), preferred_element_type=jnp.float32
    )
    return (mixed.reshape(query.shape).astype(jnp.bfloat16), log_total)


def wide_attend_backward(grad_mixed, query, keys, values, log_total, first_row):
    head_size = query.shape[2] // HEADS
    scores = wide_score_block(query, keys, first_row)
    weights = jnp.exp(scores - log_total)
    grad_heads = wide_split_heads(grad_mixed)
    grad_weights = jnp.einsum(
        "cqhd,ckhd->chqk", grad_heads, wide_split_heads(values), preferred_element_type=jnp.float32
    )
    grad_values = jnp.einsum(
        "chqk,cqhd->ckhd",
        weights.astype(jnp.bfloat16),
        grad_heads,
        preferred_element_type=jnp.float32,
    )
    inner = jnp.sum(weights * grad_weights, axis=-1, keepdims=True)
    grad_scores = (weights * (grad_weights - inner)).astype(jnp.bfloat16)
    grad_query = jnp.einsum(
        "chqk,ckhd->cqhd", grad_scores, wide_split_heads(keys), preferred_element_type=jnp.float32
    ) * head_size ** (-0.5)
    grad_keys = jnp.einsum(
        "chqk,cqhd->ckhd", grad_scores, wide_split_heads(query), preferred_element_type=jnp.float32
    ) * head_size ** (-0.5)
    return (
        grad_query.reshape(query.shape),
        grad_keys.reshape(keys.shape),
        grad_values.reshape(values.shape),
    )


def wide_mlp_forward(stream, norm_gain, norm_shift, w_up, b_up, w_down, b_down):
    normed = layer_norm(stream, norm_gain, norm_shift).astype(jnp.bfloat16)
    raised = wide_times_rows(normed, w_up) + b_up
    active = jax.nn.gelu(raised, approximate=False).astype(jnp.bfloat16)
    return (stream + wide_times_rows(active, w_down) + b_down, normed, raised, active)


def wide_mlp_backward(grad_stream, stream, norm_gain, norm_shift, normed, raised, active, w_up, w_down):
    grad_branch = grad_stream.astype(jnp.bfloat16)
    grad_wdown = wide_over_rows(active, grad_branch)
    grad_bdown = wide_column_sum(grad_branch)
    grad_active = wide_times_back(grad_branch, w_down)
    _, gelu_pull = jax.vjp(partial(jax.nn.gelu, approximate=False), raised)
    grad_raised = gelu_pull(grad_active)[0].astype(jnp.bfloat16)
    grad_wup = wide_over_rows(normed, grad_raised)
    grad_bup = wide_column_sum(grad_raised)
    grad_normed = wide_times_back(grad_raised, w_up)
    grad_in, grad_gain, grad_shift = norm_back(grad_normed, stream, norm_gain, norm_shift)
    return (
        grad_stream + grad_in,
        grad_wup,
        grad_bup,
        grad_wdown,
        grad_bdown,
        grad_gain,
        grad_shift,
    )


def wide_merge_stats(first_stats, second_stats):
    biggest = jnp.maximum(first_stats[0], second_stats[0])
    summed = first_stats[1] * jnp.exp(first_stats[0] - biggest) + second_stats[1] * jnp.exp(
        second_stats[0] - biggest
    )
    return (biggest, summed, first_stats[2] + second_stats[2])


def wide_spread_grads(grad_matrix):
    return lax.psum_scatter(grad_matrix, ("grp", "seq"), scatter_dimension=0, tiled=True)


def wide_on_device(
    frames,
    input_ids,
    target_ids,
    lengths,
    present,
    step_count,
    enc_params,
    enc_moment,
    enc_second,
    dec_params,
    dec_moment,
    dec_second,
    table_params,
    table_moment,
    table_second,
):
    enc_full, dec_full = (
        lax.all_gather(enc_params.astype(jnp.bfloat16), ("grp", "seq"), axis=0, tiled=True),
        lax.all_gather(dec_params.astype(jnp.bfloat16), ("grp", "seq"), axis=0, tiled=True),
    )
    table_local = lax.all_gather(table_params.astype(jnp.bfloat16), "grp", axis=0, tiled=True)
    enc_qkv, enc_wout, enc_wup, enc_wdown, positions, gains, shifts, biases, up_bias = split_flat(
        enc_full, enc_layout()
    )
    dec_qkv, dec_wout, cross_wq, cross_wkv, cross_wout, dec_wup, dec_wdown = split_flat(
        dec_full, dec_layout()
    )
    gains = gains.astype(jnp.float32)
    shifts = shifts.astype(jnp.float32)
    biases = biases.astype(jnp.float32)
    up_bias = up_bias.astype(jnp.float32)
    positions = positions.astype(jnp.float32)
    seq_size = lax.axis_size("seq")
    seq_rank = lax.axis_index("seq")
    group_rank = lax.axis_index("grp")
    clip_count = frames.shape[0]
    enc_rows = frames.shape[1]
    dec_rows = LEN // seq_size
    vocab_rows = table_local.shape[1]
    dec_first = seq_rank * dec_rows
    vocab_first = seq_rank * vocab_rows
    x_enc0 = (
        frames.astype(jnp.float32)
        + wide_sinusoid(enc_rows, D, (seq_rank * enc_rows).astype(jnp.float32))[None]
    )
    h_enc1 = layer_norm(x_enc0, gains[0], shifts[0]).astype(jnp.bfloat16)
    packed = wide_times_rows(h_enc1, enc_qkv)
    q_enc = (packed[..., :D] + biases[0]).astype(jnp.bfloat16)
    k_enc = packed[..., D : 2 * D].astype(jnp.bfloat16)
    v_enc = (packed[..., 2 * D :] + biases[1]).astype(jnp.bfloat16)
    keys_enc, vals_enc = (
        lax.all_gather(k_enc, "seq", axis=1, tiled=True),
        lax.all_gather(v_enc, "seq", axis=1, tiled=True),
    )
    o_enc, lse_enc = wide_attend_forward(q_enc, keys_enc, vals_enc, None)
    x_enc1 = x_enc0 + wide_times_rows(o_enc, enc_wout) + biases[2]
    x_enc2, h_enc2, up_enc, act_enc = wide_mlp_forward(
        x_enc1, gains[1], shifts[1], enc_wup, up_bias[0], enc_wdown, biases[3]
    )
    enc_out = layer_norm(x_enc2, gains[2], shifts[2]).astype(jnp.bfloat16)
    local_ids = input_ids - vocab_first
    inside = (local_ids >= 0) & (local_ids < vocab_rows)
    safe_ids = jnp.clip(local_ids, 0, vocab_rows - 1).reshape(-1)
    looked = jnp.take(table_local, safe_ids, axis=1).astype(jnp.float32).T
    looked = jnp.where(inside.reshape(-1)[:, None], looked, 0.0).reshape(clip_count, LEN, D)
    token_emb = lax.psum_scatter(
        looked.astype(jnp.bfloat16), "seq", scatter_dimension=1, tiled=True
    ).astype(jnp.float32)
    x_dec0 = token_emb + lax.dynamic_slice_in_dim(positions, dec_first, dec_rows, 0)[None]
    h_dec1 = layer_norm(x_dec0, gains[3], shifts[3]).astype(jnp.bfloat16)
    packed = wide_times_rows(h_dec1, dec_qkv)
    q_dec = (packed[..., :D] + biases[4]).astype(jnp.bfloat16)
    k_dec = packed[..., D : 2 * D].astype(jnp.bfloat16)
    v_dec = (packed[..., 2 * D :] + biases[5]).astype(jnp.bfloat16)
    paired = wide_times_rows(enc_out, cross_wkv)
    k_cross = paired[..., :D].astype(jnp.bfloat16)
    v_cross = (paired[..., D:] + biases[8]).astype(jnp.bfloat16)
    keys_dec, vals_dec, keys_cross, vals_cross = (
        lax.all_gather(k_dec, "seq", axis=1, tiled=True),
        lax.all_gather(v_dec, "seq", axis=1, tiled=True),
        lax.all_gather(k_cross, "seq", axis=1, tiled=True),
        lax.all_gather(v_cross, "seq", axis=1, tiled=True),
    )
    o_dec, lse_dec = wide_attend_forward(q_dec, keys_dec, vals_dec, dec_first)
    x_dec1 = x_dec0 + wide_times_rows(o_dec, dec_wout) + biases[6]
    h_dec2 = layer_norm(x_dec1, gains[4], shifts[4]).astype(jnp.bfloat16)
    q_cross = (wide_times_rows(h_dec2, cross_wq) + biases[7]).astype(jnp.bfloat16)
    o_cross, lse_cross = wide_attend_forward(q_cross, keys_cross, vals_cross, None)
    x_dec2 = x_dec1 + wide_times_rows(o_cross, cross_wout) + biases[9]
    x_dec3, h_dec3, up_dec, act_dec = wide_mlp_forward(
        x_dec2, gains[5], shifts[5], dec_wup, up_bias[1], dec_wdown, biases[10]
    )
    states = layer_norm(x_dec3, gains[6], shifts[6]).astype(jnp.bfloat16)
    all_states = lax.all_gather(states, "seq", axis=1, tiled=True)
    logits = wide_times_rows(all_states, table_local)
    target_local = target_ids - vocab_first
    has_target = (target_local >= 0) & (target_local < vocab_rows)
    top_local = jnp.max(logits, axis=-1)
    total_local = jnp.sum(jnp.exp(logits - top_local[..., None]), axis=-1)
    picked_local = jnp.take_along_axis(
        logits, jnp.clip(target_local, 0, vocab_rows - 1)[..., None], axis=-1
    )[..., 0]
    picked_local = jnp.where(has_target, picked_local, 0.0)
    top_all, total_all, picked_all = wide_joined_2(
        (top_local, total_local, picked_local), "seq", wide_merge_stats
    )
    log_total = top_all + jnp.log(total_all)
    my_lengths = lax.dynamic_slice_in_dim(lengths, group_rank * clip_count, clip_count)
    my_present = lax.dynamic_slice_in_dim(present, group_rank * clip_count, clip_count)
    valid = ((jnp.arange(LEN)[None, :] < my_lengths[:, None]) & (my_present[:, None] > 0)).astype(
        jnp.float32
    )
    token_total = jnp.sum((lengths * present).astype(jnp.float32))
    token_loss = (log_total - picked_all) * valid
    loss_part = jnp.sum(lax.dynamic_slice_in_dim(token_loss, dec_first, dec_rows, 1))
    row_weight = valid / token_total
    onehot = (jnp.arange(vocab_rows)[None, None, :] == target_local[..., None]).astype(jnp.float32)
    grad_logits = (
        (jnp.exp(logits - log_total[..., None]) - onehot) * row_weight[..., None]
    ).astype(jnp.bfloat16)
    grad_states_all = wide_times_back(grad_logits, table_local)
    grad_table = wide_over_rows(all_states, grad_logits)
    grad_states = lax.psum_scatter(
        grad_states_all.astype(jnp.bfloat16), "seq", scatter_dimension=1, tiled=True
    ).astype(jnp.float32)
    grad_x3, grad_g6, grad_s6 = norm_back(grad_states, x_dec3, gains[6], shifts[6])
    grad_x2, grad_dec_up, grad_dec_bup, grad_dec_down, grad_b10, grad_g5, grad_s5 = wide_mlp_backward(
        grad_x3, x_dec2, gains[5], shifts[5], h_dec3, up_dec, act_dec, dec_wup, dec_wdown
    )
    grad_branch = grad_x2.astype(jnp.bfloat16)
    grad_cross_wout = wide_over_rows(o_cross, grad_branch)
    grad_b9 = wide_column_sum(grad_branch)
    grad_mixed = wide_times_back(grad_branch, cross_wout).astype(jnp.bfloat16)
    grad_qc, grad_kc, grad_vc = wide_attend_backward(
        grad_mixed, q_cross, keys_cross, vals_cross, lse_cross, None
    )
    grad_qc = grad_qc.astype(jnp.bfloat16)
    grad_cross_wq = wide_over_rows(h_dec2, grad_qc)
    grad_b7 = wide_column_sum(grad_qc)
    grad_in, grad_g4, grad_s4 = norm_back(
        wide_times_back(grad_qc, cross_wq), x_dec1, gains[4], shifts[4]
    )
    grad_x1 = grad_x2 + grad_in
    grad_branch = grad_x1.astype(jnp.bfloat16)
    grad_dec_wout = wide_over_rows(o_dec, grad_branch)
    grad_b6 = wide_column_sum(grad_branch)
    grad_mixed = wide_times_back(grad_branch, dec_wout).astype(jnp.bfloat16)
    grad_qd, grad_kd, grad_vd = wide_attend_backward(
        grad_mixed, q_dec, keys_dec, vals_dec, lse_dec, dec_first
    )
    grad_kd, grad_vd, grad_kc, grad_vc = (
        lax.psum_scatter(
            grad_kd.astype(jnp.bfloat16), "seq", scatter_dimension=1, tiled=True
        ).astype(jnp.float32),
        lax.psum_scatter(
            grad_vd.astype(jnp.bfloat16), "seq", scatter_dimension=1, tiled=True
        ).astype(jnp.float32),
        lax.psum_scatter(
            grad_kc.astype(jnp.bfloat16), "seq", scatter_dimension=1, tiled=True
        ).astype(jnp.float32),
        lax.psum_scatter(
            grad_vc.astype(jnp.bfloat16), "seq", scatter_dimension=1, tiled=True
        ).astype(jnp.float32),
    )
    grad_qd = grad_qd.astype(jnp.bfloat16)
    grad_vd = grad_vd.astype(jnp.bfloat16)
    grad_packed = jnp.concatenate([grad_qd, grad_kd.astype(jnp.bfloat16), grad_vd], axis=-1)
    grad_dec_qkv = wide_over_rows(h_dec1, grad_packed)
    grad_b4 = wide_column_sum(grad_qd)
    grad_b5 = wide_column_sum(grad_vd)
    grad_in, grad_g3, grad_s3 = norm_back(
        wide_times_back(grad_packed, dec_qkv), x_dec0, gains[3], shifts[3]
    )
    grad_x0 = grad_x1 + grad_in
    grad_positions = lax.dynamic_update_slice_in_dim(
        jnp.zeros((LEN, D), jnp.float32), jnp.sum(grad_x0, axis=0), dec_first, 0
    )
    grad_embed_all = lax.all_gather(grad_x0.astype(jnp.bfloat16), "seq", axis=1, tiled=True).astype(
        grad_x0.dtype
    )
    grad_embed_all = jnp.where(inside.reshape(-1)[:, None], grad_embed_all.reshape(-1, D), 0.0)
    grad_table = grad_table.at[:, safe_ids].add(grad_embed_all.T)
    grad_vc = grad_vc.astype(jnp.bfloat16)
    grad_pair = jnp.concatenate([grad_kc.astype(jnp.bfloat16), grad_vc], axis=-1)
    grad_cross_wkv = wide_over_rows(enc_out, grad_pair)
    grad_b8 = wide_column_sum(grad_vc)
    grad_enc2, grad_g2, grad_s2 = norm_back(
        wide_times_back(grad_pair, cross_wkv), x_enc2, gains[2], shifts[2]
    )
    device_count = lax.axis_size(("grp", "seq"))
    dec_flat = jnp.concatenate(
        [
            grad_dec_qkv.reshape(-1),
            grad_dec_wout.reshape(-1),
            grad_cross_wq.reshape(-1),
            grad_cross_wkv.reshape(-1),
            grad_cross_wout.reshape(-1),
            grad_dec_up.reshape(-1),
            grad_dec_down.reshape(-1),
        ]
    )
    dec_matrix = dec_flat.reshape(device_count, -1)
    dec_columns = dec_matrix.shape[1]
    grad_enc1, grad_enc_up, grad_enc_bup, grad_enc_down, grad_b3, grad_g1, grad_s1 = wide_mlp_backward(
        grad_enc2, x_enc1, gains[1], shifts[1], h_enc2, up_enc, act_enc, enc_wup, enc_wdown
    )
    grad_branch = grad_enc1.astype(jnp.bfloat16)
    grad_enc_wout = wide_over_rows(o_enc, grad_branch)
    grad_b2 = wide_column_sum(grad_branch)
    grad_mixed = wide_times_back(grad_branch, enc_wout).astype(jnp.bfloat16)
    grad_qe, grad_ke, grad_ve = wide_attend_backward(
        grad_mixed, q_enc, keys_enc, vals_enc, lse_enc, None
    )
    grad_ke, grad_ve = (
        lax.psum_scatter(
            grad_ke.astype(jnp.bfloat16), "seq", scatter_dimension=1, tiled=True
        ).astype(jnp.float32),
        lax.psum_scatter(
            grad_ve.astype(jnp.bfloat16), "seq", scatter_dimension=1, tiled=True
        ).astype(jnp.float32),
    )
    grad_qe = grad_qe.astype(jnp.bfloat16)
    grad_ve = grad_ve.astype(jnp.bfloat16)
    grad_packed = jnp.concatenate([grad_qe, grad_ke.astype(jnp.bfloat16), grad_ve], axis=-1)
    grad_enc_qkv = wide_over_rows(h_enc1, grad_packed)
    grad_b0 = wide_column_sum(grad_qe)
    grad_b1 = wide_column_sum(grad_ve)
    _, grad_g0, grad_s0 = norm_back(
        wide_times_back(grad_packed, enc_qkv), x_enc0, gains[0], shifts[0]
    )
    grad_gains = jnp.stack([grad_g0, grad_g1, grad_g2, grad_g3, grad_g4, grad_g5, grad_g6])
    grad_shifts = jnp.stack([grad_s0, grad_s1, grad_s2, grad_s3, grad_s4, grad_s5, grad_s6])
    grad_biases = jnp.stack(
        [
            grad_b0,
            grad_b1,
            grad_b2,
            grad_b3,
            grad_b4,
            grad_b5,
            grad_b6,
            grad_b7,
            grad_b8,
            grad_b9,
            grad_b10,
        ]
    )
    grad_up_bias = jnp.stack([grad_enc_bup, grad_dec_bup])
    enc_flat = jnp.concatenate(
        [
            grad_enc_qkv.reshape(-1),
            grad_enc_wout.reshape(-1),
            grad_enc_up.reshape(-1),
            grad_enc_down.reshape(-1),
            grad_positions.reshape(-1),
            grad_gains.reshape(-1),
            grad_shifts.reshape(-1),
            grad_biases.reshape(-1),
            grad_up_bias.reshape(-1),
        ]
    )
    enc_matrix = enc_flat.reshape(device_count, -1)
    joined = wide_spread_grads(jnp.concatenate([dec_matrix, enc_matrix], axis=1))
    dec_grad = joined[:, :dec_columns].reshape(-1)
    enc_grad = joined[:, dec_columns:].reshape(-1)
    table_grad = lax.psum_scatter(grad_table, "grp", scatter_dimension=0, tiled=True)
    squares = (
        jnp.sum(enc_grad * enc_grad)
        + jnp.sum(dec_grad * dec_grad)
        + jnp.sum(table_grad * table_grad)
    )
    loss_sum, square_sum = lax.psum((loss_part, squares), ("grp", "seq"))
    mean_loss = loss_sum / token_total
    grad_norm = jnp.sqrt(square_sum)
    factor = jnp.minimum(1.0, clip_limit / (grad_norm + 1e-06))
    steps_done = step_count[0].astype(jnp.float32)
    bias_one = 1.0 - beta_one**steps_done
    bias_two = 1.0 - beta_two**steps_done
    enc_new = adamw(enc_params, enc_moment, enc_second, enc_grad, factor, bias_one, bias_two)
    dec_new = adamw(dec_params, dec_moment, dec_second, dec_grad, factor, bias_one, bias_two)
    table_new = adamw(
        table_params, table_moment, table_second, table_grad, factor, bias_one, bias_two
    )
    return (
        mean_loss,
        grad_norm,
        enc_new[0],
        enc_new[1],
        enc_new[2],
        dec_new[0],
        dec_new[1],
        dec_new[2],
        table_new[0],
        table_new[1],
        table_new[2],
    )


def solution(mesh):
    flat = P(("grp", "seq"))
    both = P("grp", "seq")
    in_specs = (
        P("grp", "seq", None),
        P("grp", None),
        P("grp", None),
        P(),
        P(),
        P(),
        flat,
        flat,
        flat,
        flat,
        flat,
        flat,
        both,
        both,
        both,
    )
    out_specs = (P(), P(), flat, flat, flat, flat, flat, flat, both, both, both)
    few = mesh.shape["grp"] == 8
    return jax.shard_map(
        on_device if few else wide_on_device,
        mesh=mesh,
        in_specs=in_specs,
        out_specs=out_specs,
        check_vma=False,
    )
```

profile of v0, /device:TPU:0, one launch (start us, length us, event | category | flops | bytes accessed | tf_op | source)
XLA Modules:
  0.0 938.4 jit_solution(1213557300602556183)
XLA Ops:
  32.1 7.0 multiply_sine_fusion.2
  44.8 8.5 collective-permute-done.21
  58.1 9.3 collective-permute-done.20
  118.3 8.1 fusion.9
  148.1 8.5 collective-permute-done.25
  169.3 29.2 %collective-permute-done.10 = bf16[2,224,512]{2,1,0:T(8,128)(2,1)S(1)} collective-permute-done((bf16[2,224,512]{2,1,0:T(8,128)(2,1)S(1)}, bf16[2,224,512]{2,1,0:T(8,128)(2,1)S(1)}, u32[]{:S(2)}, u32[]{:S(2)}) %collective-permute-start.10) | collective-permute-done | bytes 458784 | tf_op jit(solution)/shard_map/ppermute | solution.py:84
  214.2 9.7 %lay_out.2 = (bf16[512,1536]{1,0:T(8,128)(2,1)}, bf16[512,512]{1,0:T(8,128)(2,1)}, bf16[512,2048]{1,0:T(8,128)(2,1)}, bf16[2048,512]{1,0:T(8,128)(2,1)}, bf16[44...) custom-call(s32[1]{0:T(128)} %bitcast.23.rank_ref, bf16[4,4,416,128]{3,2,1,0:T(8,128)(2,1)} %copy-done.26, ...), custom_call_target="tpu_custom_call" | custom-call | tf_op jit(solution)/shard_map/lay_out/pallas_call | solution.py:254
  231.8 17.3 %attend_forward.4 = (bf16[1536,128]{1,0:T(8,128)(2,1)}, f32[2,1536]{1,0:T(2,128)}) custom-call(bf16[1536,128]{1,0:T(8,128)(2,1)} %get-tuple-element.198.query_ref, bf16[1536,128]{1,0:T(8,128)(2,1)} %slice.1707.key_ref, bf16[1536,128]{1,0:T(8,128)(2,1)} %get-tuple-element.197.value_ref, f32[1536,1]{1,0:T(8,128)} %fusion.49.bias_ref), custom_call_target="tpu_custom_call" | custom-call | tf_op jit(solution)/shard_map/attend_forward/pallas_call | solution.py:415
  267.9 9.5 %multiply_convert_fusion.1 = (bf16[384,2048]{1,0:T(8,128)(2,1)S(1)}, f32[384,2048]{1,0:T(8,128)}, f32[384,2048]{1,0:T(8,128)}) fusion(f32[2048]{0:T(1024)S(1)} %get-tuple-element.369, bf16[384,512]{1,0:T(8,128)(2,1)S(1)} %add_convert_fusion.11.refs_0_, bf16[512,2048]{1,0:T(8,128)(2,1)S(1)} %copy-done.232), kind=kOutput, calls=%fused_computation.42 | convolution fusion | flops 857210880 | bytes 10362880 | tf_op jit(solution)/shard_map/dot_general | solution.py:63
  292.1 11.6 %lay_out.3 = (bf16[512,1536]{1,0:T(8,128)(2,1)}, bf16[512,512]{1,0:T(8,128)(2,1)}, bf16[512,512]{1,0:T(8,128)(2,1)}, bf16[512,1024]{1,0:T(8,128)(2,1)}, bf16[512...) custom-call(s32[1]{0:T(128)} %bitcast.23.rank_ref, ...), custom_call_target="tpu_custom_call" | custom-call | tf_op jit(solution)/shard_map/lay_out/pallas_call | solution.py:254
  350.8 10.5 %multiply_convert_fusion = (bf16[448,2048]{1,0:T(8,128)(2,1)S(1)}, f32[448,2048]{1,0:T(8,128)}, f32[448,2048]{1,0:T(8,128)}) fusion(f32[2048]{0:T(1024)S(1)} %copy-done.203, bf16[448,512]{1,0:T(8,128)(2,1)S(1)} %add_convert_fusion.5.refs_8_, bf16[512,2048]{1,0:T(8,128)(2,1)S(1)} %copy-done.235), kind=kOutput, calls=%fused_computation.17 | convolution fusion | flops 1000079360 | bytes 11739136 | tf_op jit(solution)/shard_map/dot_general | solution.py:63
  372.7 8.9 collective-permute-done.52
  383.3 7.0 collective-permute-done.53
  398.7 16.7 %loss_forward.1.refs_0_ = f32[8,8,448]{2,1,0:T(8,128)} custom-call(s32[1]{0:T(128)} %bitcast.rank_ref, s32[1]{0:T(128)} %bitcast.1.here_ref, bf16[8,448,512]{2,1,0:T(8,128)(2,1)} %fusion.91.states_ref, bf16[512,1664]{1,0:T(8,128)(2,1)} %copy-done.20, s32[8,1,448]{2,1,0:T(1,128)} %get-tuple-element.376.target_ref), custom_call_target="tpu_custom_call" | custom-call | tf_op jit(solution)/shard_map/loss_forward/pallas_call | solution.py:537
  451.5 20.5 %loss_backward.1 = (bf16[8,448,1664]{2,1,0:T(8,128)(2,1)}, f32[8,448,512]{2,1,0:T(8,128)}) custom-call(s32[1]{0:T(128)} %bitcast.rank_ref, s32[1]{0:T(128)} %bitcast.1.here_ref, bf16[8,448,512]{2,1,0:T(8,128)(2,1)} %fusion.91.states_ref, bf16[512,1664]{1,0:T(8,128)(2,1)} %copy-done.20, s32[8,1,448]{2,1,0:T(1,128)} %get-tuple-element.376.target_ref, ...), custom_call_target="tpu_custom_call" | custom-call | tf_op jit(solution)/shard_map/loss_backward/pallas_call | solution.py:616
  488.4 7.8 collective-permute-done.67
  512.0 13.2 %convolution_bitcast_fusion = f32[512,1664]{1,0:T(8,128)} fusion(bf16[8,448,512]{2,1,0:T(8,128)(2,1)} %fusion.91.states_ref, bf16[8,448,1664]{2,1,0:T(8,128)(2,1)} %get-tuple-element.70), kind=kOutput, calls=%fused_computation.35 | convolution fusion | flops 6106906624 | bytes 19005440 | tf_op jit(solution)/shard_map/dot_general | solution.py:73
  552.0 7.1 attend_backward.3
  642.7 19.4 %attend_backward.5 = (bf16[1536,128]{1,0:T(8,128)(2,1)}, bf16[1536,128]{1,0:T(8,128)(2,1)}, bf16[1536,128]{1,0:T(8,128)(2,1)}) custom-call(bf16[1536,128]{1,0:T(8,128)(2,1)} %pad_maximum_fusion.32.grad_ref, bf16[1536,128]{1,0:T(8,128)(2,1)} %get-tuple-element.198.query_ref, bf16[1536,128]{1,0:T(8,128)(2,1)} %slice.1707.key_ref, ...), custom_call_target="tpu_custom_call" | custom-call | tf_op jit(solution)/shard_map/attend_backward/pallas_call | solution.py:481
  689.9 7.3 constant_dynamic-slice_fusion.23
  702.4 7.8 own_blocks.1
  726.0 10.7 %fusion.20 = f32[512,1664]{1,0:T(8,128)S(1)} fusion(f32[512,1664]{1,0:T(8,128)} %convolution_bitcast_fusion, bf16[3584,512]{1,0:T(8,128)(2,1)} %bitcast.615, s32[3584]{0:T(1024)S(1)} %copy-done.184, pred[1664]{0:T(1024)(128)(4,1)S(1)} %copy-done.219), kind=kOutput, calls=%fused_computation.36 | convolution fusion | flops 6119686144 | bytes 10501760 | tf_op jit(solution)/shard_map/dot_general | solution.py:73
  742.4 8.3 collective-permute-done.115
  759.7 8.1 collective-permute-done.118
  768.9 7.5 collective-permute-done.114
  782.7 9.8 %collective-permute-done.106 = f32[1,2,512,128]{3,2,1,0:T(8,128)S(1)} collective-permute-done((f32[1,2,512,128]{3,2,1,0:T(8,128)S(1)}, f32[1,2,512,128]{3,2,1,0:T(8,128)S(1)}, u32[]{:S(2)}, u32[]{:S(2)}) %collective-permute-start.106) | collective-permute-done | bytes 524320 | tf_op jit(solution)/shard_map/ppermute | solution.py:84
  800.3 19.7 %collective-permute-done.88 = f32[2,1,2,416,128]{4,3,2,1,0:T(8,128)S(1)} collective-permute-done((f32[2,1,2,416,128]{4,3,2,1,0:T(8,128)S(1)}, f32[2,1,2,416,128]{4,3,2,1,0:T(8,128)S(1)}, u32[]{:S(2)}, u32[]{:S(2)}) %collective-permute-start.88) | collective-permute-done | bytes 852000 | tf_op jit(solution)/shard_map/ppermute | solution.py:84
  824.1 12.8 %collective-permute-done.94 = f32[2,1,2,416,128]{4,3,2,1,0:T(8,128)S(1)} collective-permute-done((f32[2,1,2,416,128]{4,3,2,1,0:T(8,128)S(1)}, f32[2,1,2,416,128]{4,3,2,1,0:T(8,128)S(1)}, u32[]{:S(2)}, u32[]{:S(2)}) %collective-permute-start.94) | collective-permute-done | bytes 852000 | tf_op jit(solution)/shard_map/ppermute | solution.py:84
  843.2 7.8 collective-permute-done.89
  863.4 10.5 %collective-permute-done.99 = f32[832,128]{1,0:T(8,128)S(1)} collective-permute-done((f32[832,128]{1,0:T(8,128)S(1)}, f32[832,128]{1,0:T(8,128)S(1)}, u32[]{:S(2)}, u32[]{:S(2)}) %collective-permute-start.99) | collective-permute-done | bytes 426016 | tf_op jit(solution)/shard_map/ppermute | solution.py:84
  873.9 22.4 %collective-permute-done.98 = f32[832,128]{1,0:T(8,128)S(1)} collective-permute-done((f32[832,128]{1,0:T(8,128)S(1)}, f32[832,128]{1,0:T(8,128)S(1)}, u32[]{:S(2)}, u32[]{:S(2)}) %collective-permute-start.98) | collective-permute-done | bytes 426016 | tf_op jit(solution)/shard_map/ppermute | solution.py:84
  927.7 6.7 multiply_subtract_fusion
  (1110 shorter events, 553.3 us)
Async XLA Ops:
  2.6 72.0 %collective-permute-start.30 = (bf16[1024,128]{1,0:T(8,128)(2,1)}, bf16[1024,128]{1,0:T(8,128)(2,1)}, u32[]{:S(2)}, u32[]{:S(2)}) collective-permute-start(bf16[1024,128]{1,0:T(8,128)(2,1)} %convert_bitcast_fusion), channel_id=1, source_target_pairs={{0,3},{1,2},{2,1},{3,0},{4,7},{5,6},{6,5},{7,4},{8,11},{9,10},{10,... | collective-permute-start | bytes 786440 | tf_op jit(solution)/shard_map/ppermute | solution.py:84
  7.7 68.8 %collective-permute-start.29 = (bf16[1024,128]{1,0:T(8,128)(2,1)}, bf16[1024,128]{1,0:T(8,128)(2,1)}, u32[]{:S(2)}, u32[]{:S(2)}) collective-permute-start(bf16[1024,128]{1,0:T(8,128)(2,1)} %convert_bitcast_fusion), channel_id=1, source_target_pairs={{0,2},{1,3},{2,0},{3,1},{4,6},{5,7},{6,4},{7,5},{8,10},{9,11},{10,... | collective-permute-start | bytes 786440 | tf_op jit(solution)/shard_map/ppermute | solution.py:84
  7.7 73.0 %collective-permute-start.28 = (bf16[1024,128]{1,0:T(8,128)(2,1)}, bf16[1024,128]{1,0:T(8,128)(2,1)}, u32[]{:S(2)}, u32[]{:S(2)}) collective-permute-start(bf16[1024,128]{1,0:T(8,128)(2,1)} %convert_bitcast_fusion), channel_id=1, source_target_pairs={{0,1},{1,0},{2,3},{3,2},{4,5},{5,4},{6,7},{7,6},{8,9},{9,8},{10,11... | collective-permute-start | bytes 786440 | tf_op jit(solution)/shard_map/ppermute | solution.py:84
  9.9 32.1 %collective-permute-start.18 = (bf16[15872]{0:T(1024)(128)(2,1)}, bf16[15872]{0:T(1024)(128)(2,1)}, u32[]{:S(2)}, u32[]{:S(2)}) collective-permute-start(bf16[15872]{0:T(1024)(128)(2,1)} %slice.1112), channel_id=1, source_target_pairs={{1,0},{2,1},{3,2},{4,3},{5,4},{6,5},{7,6},{8,7},{9,8},{10,9},{11,1... | collective-permute-start | bytes 95240 | tf_op jit(solution)/shard_map/ppermute | solution.py:767
  12.9 123.6 %collective-permute-start.41 = (bf16[384,512]{1,0:T(8,128)(2,1)}, bf16[384,512]{1,0:T(8,128)(2,1)}, u32[]{:S(2)}, u32[]{:S(2)}) collective-permute-start(bf16[384,512]{1,0:T(8,128)(2,1)} %pad.18), channel_id=1, source_target_pairs={{0,2},{1,3},{2,0},{3,1},{4,6},{5,7},{6,4},{7,5},{8,10},{9,11},{10,... | collective-permute-start | bytes 1179656 | tf_op jit(solution)/shard_map/ppermute | solution.py:84
  73.3 54.4 %collective-permute-start.40 = (bf16[384,512]{1,0:T(8,128)(2,1)}, bf16[384,512]{1,0:T(8,128)(2,1)}, u32[]{:S(2)}, u32[]{:S(2)}) collective-permute-start(bf16[384,512]{1,0:T(8,128)(2,1)} %pad.18), channel_id=1, source_target_pairs={{0,1},{1,0},{2,3},{3,2},{4,5},{5,4},{6,7},{7,6},{8,9},{9,8},{10,11... | collective-permute-start | bytes 1179656 | tf_op jit(solution)/shard_map/ppermute | solution.py:84
  102.2 32.5 %collective-permute-start.22 = (bf16[1,4,416,128]{3,2,1,0:T(8,128)(2,1)S(1)}, bf16[1,4,416,128]{3,2,1,0:T(8,128)(2,1)}, u32[]{:S(2)}, u32[]{:S(2)}) collective-permute-start(bf16[1,4,416,128]{3,2,1,0:T(8,128)(2,1)S(1)} %maximum_bitcast_fusion.16), channel_id=1, source_target_pairs={{0,8},{4,12},{8,0},{12,4},{16,24},{20,28},{24,16},{28,20},{1,9},{5... | collective-permute-start | bytes 1277960 | tf_op jit(solution)/shard_map/ppermute | solution.py:84
  126.8 38.3 %collective-permute-start.7 = (bf16[4,448,512]{2,1,0:T(8,128)(2,1)S(1)}, bf16[4,448,512]{2,1,0:T(8,128)(2,1)S(1)}, u32[]{:S(2)}, u32[]{:S(2)}) collective-permute-start(bf16[4,448,512]{2,1,0:T(8,128)(2,1)S(1)} %pad_maximum_fusion.3), channel_id=1, source_target_pairs={{0,4},{4,0},{8,12},{12,8},{16,20},{20,16},{24,28},{28,24},{1,5},{5... | collective-permute-start | bytes 5505032 | tf_op jit(solution)/shard_map/ppermute | solution.py:84
  147.0 53.1 %collective-permute-start.34 = (bf16[2,4,512,128]{3,2,1,0:T(8,128)(2,1)S(1)}, bf16[2,4,512,128]{3,2,1,0:T(8,128)(2,1)S(1)}, u32[]{:S(2)}, u32[]{:S(2)}) collective-permute-start(bf16[2,4,512,128]{3,2,1,0:T(8,128)(2,1)S(1)} %pad_maximum_fusion.8), channel_id=1, source_target_pairs={{0,8},{4,12},{8,0},{12,4},{16,24},{20,28},{24,16},{28,20},{1,9},{5... | collective-permute-start | bytes 3145736 | tf_op jit(solution)/shard_map/ppermute | solution.py:84
  157.9 53.9 %collective-permute-start.27 = (bf16[4,4,416,128]{3,2,1,0:T(8,128)(2,1)S(1)}, bf16[4,4,416,128]{3,2,1,0:T(8,128)(2,1)S(1)}, u32[]{:S(2)}, u32[]{:S(2)}) collective-permute-start(bf16[4,4,416,128]{3,2,1,0:T(8,128)(2,1)S(1)} %pad_maximum_fusion.6.own_b), channel_id=1, source_target_pairs={{0,4},{4,0},{8,12},{12,8},{16,20},{20,16},{24,28},{28,24},{1,5},{5... | collective-permute-start | bytes 5111816 | tf_op jit(solution)/shard_map/ppermute | solution.py:84
  165.0 47.7 %collective-permute-start.26 = (bf16[4,4,416,128]{3,2,1,0:T(8,128)(2,1)S(1)}, bf16[4,4,416,128]{3,2,1,0:T(8,128)(2,1)S(1)}, u32[]{:S(2)}, u32[]{:S(2)}) collective-permute-start(bf16[4,4,416,128]{3,2,1,0:T(8,128)(2,1)S(1)} %pad_maximum_fusion.5.own_a), channel_id=1, source_target_pairs={{0,4},{4,0},{8,12},{12,8},{16,20},{20,16},{24,28},{28,24},{1,5},{5... | collective-permute-start | bytes 5111816 | tf_op jit(solution)/shard_map/ppermute | solution.py:84
  166.4 32.1 %collective-permute-start.10 = (bf16[2,224,512]{2,1,0:T(8,128)(2,1)S(1)}, bf16[2,224,512]{2,1,0:T(8,128)(2,1)S(1)}, u32[]{:S(2)}, u32[]{:S(2)}) collective-permute-start(bf16[2,224,512]{2,1,0:T(8,128)(2,1)S(1)} %pad_maximum_fusion.18), channel_id=1, source_target_pairs={{0,8},{4,12},{8,0},{12,4},{16,24},{20,28},{24,16},{28,20},{1,9},{5... | collective-permute-start | bytes 1376264 | tf_op jit(solution)/shard_map/ppermute | solution.py:84
  167.9 33.8 %collective-permute-start.32 = (bf16[2,4,512,128]{3,2,1,0:T(8,128)(2,1)S(1)}, bf16[2,4,512,128]{3,2,1,0:T(8,128)(2,1)S(1)}, u32[]{:S(2)}, u32[]{:S(2)}) collective-permute-start(bf16[2,4,512,128]{3,2,1,0:T(8,128)(2,1)S(1)} %pad_maximum_fusion.7), channel_id=1, source_target_pairs={{0,16},{4,20},{8,24},{12,28},{16,0},{20,4},{24,8},{28,12},{1,17},{... | collective-permute-start | bytes 3145736 | tf_op jit(solution)/shard_map/ppermute | solution.py:84
  201.7 90.3 %collective-permute-start.36 = (bf16[4,4,512,128]{3,2,1,0:T(8,128)(2,1)}, bf16[4,4,512,128]{3,2,1,0:T(8,128)(2,1)}, u32[]{:S(2)}, u32[]{:S(2)}) collective-permute-start(bf16[4,4,512,128]{3,2,1,0:T(8,128)(2,1)} %pad_maximum_fusion.2.own_b), channel_id=1, source_target_pairs={{0,4},{4,0},{8,12},{12,8},{16,20},{20,16},{24,28},{28,24},{1,5},{5... | collective-permute-start | bytes 6291464 | tf_op jit(solution)/shard_map/ppermute | solution.py:84
  203.3 88.7 %collective-permute-start.35 = (bf16[4,4,512,128]{3,2,1,0:T(8,128)(2,1)}, bf16[4,4,512,128]{3,2,1,0:T(8,128)(2,1)}, u32[]{:S(2)}, u32[]{:S(2)}) collective-permute-start(bf16[4,4,512,128]{3,2,1,0:T(8,128)(2,1)} %pad_maximum_fusion.1.own_a), channel_id=1, source_target_pairs={{0,4},{4,0},{8,12},{12,8},{16,20},{20,16},{24,28},{28,24},{1,5},{5... | collective-permute-start | bytes 6291464 | tf_op jit(solution)/shard_map/ppermute | solution.py:84
  210.3 43.7 %collective-permute-start.11 = (bf16[1,224,512]{2,1,0:T(8,128)(2,1)}, bf16[1,224,512]{2,1,0:T(8,128)(2,1)S(1)}, u32[]{:S(2)}, u32[]{:S(2)}) collective-permute-start(bf16[1,224,512]{2,1,0:T(8,128)(2,1)} %get-tuple-element.310), channel_id=1, source_target_pairs={{0,16},{4,20},{8,24},{12,28},{16,0},{20,4},{24,8},{28,12},{1,17},{... | collective-permute-start | bytes 688136 | tf_op jit(solution)/shard_map/ppermute | solution.py:84
  211.8 42.6 %collective-permute-start.9 = (bf16[1,224,512]{2,1,0:T(8,128)(2,1)}, bf16[1,224,512]{2,1,0:T(8,128)(2,1)}, u32[]{:S(2)}, u32[]{:S(2)}) collective-permute-start(bf16[1,224,512]{2,1,0:T(8,128)(2,1)} %fusion.125), channel_id=1, source_target_pairs={{0,8},{4,12},{8,0},{12,4},{16,24},{20,28},{24,16},{28,20},{1,9},{5... | collective-permute-start | bytes 688136 | tf_op jit(solution)/shard_map/ppermute | solution.py:84
  588.9 87.1 %collective-permute-start.80 = (bf16[448,384]{1,0:T(8,128)(2,1)}, bf16[448,384]{1,0:T(8,128)(2,1)}, u32[]{:S(2)}, u32[]{:S(2)}) collective-permute-start(bf16[448,384]{1,0:T(8,128)(2,1)} %constant_dynamic-update-slice_fusion), channel_id=1, source_target_pairs={{0,1},{1,0},{2,3},{3,2},{4,5},{5,4},{6,7},{7,6},{8,9},{9,8},{10,11... | collective-permute-start | bytes 1032200 | tf_op jit(solution)/shard_map/ppermute | solution.py:84
  591.2 86.8 %collective-permute-start.79 = (bf16[448,384]{1,0:T(8,128)(2,1)}, bf16[448,384]{1,0:T(8,128)(2,1)}, u32[]{:S(2)}, u32[]{:S(2)}) collective-permute-start(bf16[448,384]{1,0:T(8,128)(2,1)} %constant_dynamic-update-slice_fusion), channel_id=1, source_target_pairs={{0,2},{1,3},{2,0},{3,1},{4,6},{5,7},{6,4},{7,5},{8,10},{9,11},{10,... | collective-permute-start | bytes 1032200 | tf_op jit(solution)/shard_map/ppermute | solution.py:84
  638.0 40.1 %collective-permute-start.78 = (bf16[448,384]{1,0:T(8,128)(2,1)}, bf16[448,384]{1,0:T(8,128)(2,1)}, u32[]{:S(2)}, u32[]{:S(2)}) collective-permute-start(bf16[448,384]{1,0:T(8,128)(2,1)} %constant_dynamic-update-slice_fusion), channel_id=1, source_target_pairs={{0,3},{1,2},{2,1},{3,0},{4,7},{5,6},{6,5},{7,4},{8,11},{9,10},{10,... | collective-permute-start | bytes 1032200 | tf_op jit(solution)/shard_map/ppermute | solution.py:84
  640.3 72.8 %collective-permute-start.100 = (f32[1024,128]{1,0:T(8,128)}, f32[1024,128]{1,0:T(8,128)}, u32[]{:S(2)}, u32[]{:S(2)}) collective-permute-start(f32[1024,128]{1,0:T(8,128)} %get-tuple-element.208), channel_id=1, source_target_pairs={{0,1},{1,0},{2,3},{3,2},{4,5},{5,4},{6,7},{7,6},{8,9},{9,8},{10,11... | collective-permute-start | bytes 1572872 | tf_op jit(solution)/shard_map/ppermute | solution.py:84
  640.6 72.5 %collective-permute-start.102 = (f32[1024,128]{1,0:T(8,128)}, f32[1024,128]{1,0:T(8,128)}, u32[]{:S(2)}, u32[]{:S(2)}) collective-permute-start(f32[1024,128]{1,0:T(8,128)} %get-tuple-element.209), channel_id=1, source_target_pairs={{0,3},{1,2},{2,1},{3,0},{4,7},{5,6},{6,5},{7,4},{8,11},{9,10},{10,... | collective-permute-start | bytes 1572872 | tf_op jit(solution)/shard_map/ppermute | solution.py:84
  676.0 37.1 %collective-permute-start.101 = (f32[1024,128]{1,0:T(8,128)}, f32[1024,128]{1,0:T(8,128)}, u32[]{:S(2)}, u32[]{:S(2)}) collective-permute-start(f32[1024,128]{1,0:T(8,128)} %get-tuple-element.210), channel_id=1, source_target_pairs={{0,2},{1,3},{2,0},{3,1},{4,6},{5,7},{6,4},{7,5},{8,10},{9,11},{10,... | collective-permute-start | bytes 1572872 | tf_op jit(solution)/shard_map/ppermute | solution.py:84
  740.0 27.8 %collective-permute-start.118 = (f32[64,1664]{1,0:T(8,128)S(1)}, f32[64,1664]{1,0:T(8,128)S(1)}, u32[]{:S(2)}, u32[]{:S(2)}) collective-permute-start(f32[64,1664]{1,0:T(8,128)S(1)} %get-tuple-element.189), channel_id=1, source_target_pairs={{0,12},{4,8},{8,4},{12,0},{16,28},{20,24},{24,20},{28,16},{1,13},{... | collective-permute-start | bytes 1277960 | tf_op jit(solution)/shard_map/ppermute | solution.py:84
  759.7 34.7 %collective-permute-start.87 = (f32[2,2,2,832,128]{4,3,2,1,0:T(8,128)}, f32[2,2,2,832,128]{4,3,2,1,0:T(8,128)S(1)}, u32[]{:S(2)}, u32[]{:S(2)}) collective-permute-start(f32[2,2,2,832,128]{4,3,2,1,0:T(8,128)} %bitcast.134), channel_id=1, source_target_pairs={{0,4},{4,0},{8,12},{12,8},{16,20},{20,16},{24,28},{28,24},{1,5},{5... | collective-permute-start | bytes 10223624 | tf_op jit(solution)/shard_map/ppermute | solution.py:84
  767.8 30.4 %collective-permute-start.93 = (f32[2,2,2,832,128]{4,3,2,1,0:T(8,128)}, f32[2,2,2,832,128]{4,3,2,1,0:T(8,128)S(1)}, u32[]{:S(2)}, u32[]{:S(2)}) collective-permute-start(f32[2,2,2,832,128]{4,3,2,1,0:T(8,128)} %bitcast.141), channel_id=1, source_target_pairs={{0,4},{4,0},{8,12},{12,8},{16,20},{20,16},{24,28},{28,24},{1,5},{5... | collective-permute-start | bytes 10223624 | tf_op jit(solution)/shard_map/ppermute | solution.py:84
  792.6 69.3 %collective-permute-start.107 = (f32[1,1,512,128]{3,2,1,0:T(8,128)S(1)}, f32[1,1,512,128]{3,2,1,0:T(8,128)S(1)}, u32[]{:S(2)}, u32[]{:S(2)}) collective-permute-start(f32[1,1,512,128]{3,2,1,0:T(8,128)S(1)} %constant_dynamic-slice_fusion.7), channel_id=1, source_target_pairs={{0,8},{4,12},{8,0},{12,4},{16,24},{20,28},{24,16},{28,20},{1,9},{5... | collective-permute-start | bytes 786440 | tf_op jit(solution)/shard_map/ppermute | solution.py:84
  796.0 65.9 %collective-permute-start.105 = (f32[1,1,512,128]{3,2,1,0:T(8,128)S(1)}, f32[1,1,512,128]{3,2,1,0:T(8,128)S(1)}, u32[]{:S(2)}, u32[]{:S(2)}) collective-permute-start(f32[1,1,512,128]{3,2,1,0:T(8,128)S(1)} %constant_dynamic-slice_fusion.9), channel_id=1, source_target_pairs={{0,16},{4,20},{8,24},{12,28},{16,0},{20,4},{24,8},{28,12},{1,17},{... | collective-permute-start | bytes 786440 | tf_op jit(solution)/shard_map/ppermute | solution.py:84
  799.0 38.0 %collective-permute-start.94 = (f32[2,1,2,416,128]{4,3,2,1,0:T(8,128)S(1)}, f32[2,1,2,416,128]{4,3,2,1,0:T(8,128)S(1)}, u32[]{:S(2)}, u32[]{:S(2)}) collective-permute-start(f32[2,1,2,416,128]{4,3,2,1,0:T(8,128)S(1)} %constant_dynamic-slice_fusion.16), channel_id=1, source_target_pairs={{0,8},{4,12},{8,0},{12,4},{16,24},{20,28},{24,16},{28,20},{1,9},{5... | collective-permute-start | bytes 2555912 | tf_op jit(solution)/shard_map/ppermute | solution.py:84
  823.0 28.0 %collective-permute-start.89 = (f32[1,1,2,416,128]{4,3,2,1,0:T(8,128)S(1)}, f32[1,1,2,416,128]{4,3,2,1,0:T(8,128)S(1)}, u32[]{:S(2)}, u32[]{:S(2)}) collective-permute-start(f32[1,1,2,416,128]{4,3,2,1,0:T(8,128)S(1)} %constant_dynamic-slice_fusion.21), channel_id=1, source_target_pairs={{0,16},{4,20},{8,24},{12,28},{16,0},{20,4},{24,8},{28,12},{1,17},{... | collective-permute-start | bytes 1277960 | tf_op jit(solution)/shard_map/ppermute | solution.py:84
  861.5 34.7 %collective-permute-start.98 = (f32[832,128]{1,0:T(8,128)S(1)}, f32[832,128]{1,0:T(8,128)S(1)}, u32[]{:S(2)}, u32[]{:S(2)}) collective-permute-start(f32[832,128]{1,0:T(8,128)S(1)} %get-tuple-element.247), channel_id=1, source_target_pairs={{0,2},{1,3},{2,0},{3,1},{4,6},{5,7},{6,4},{7,5},{8,10},{9,11},{10,... | collective-permute-start | bytes 1277960 | tf_op jit(solution)/shard_map/ppermute | solution.py:84
  901.4 33.1 %collective-permute-start.127 = (f32[15872]{0:T(1024)S(1)}, f32[15872]{0:T(1024)S(1)}, u32[]{:S(2)}, u32[]{:S(2)}) collective-permute-start(f32[15872]{0:T(1024)S(1)} %slice_bitcast_fusion.64), channel_id=1, source_target_pairs={{0,1},{1,2},{2,3},{3,4},{4,5},{5,6},{6,7},{7,8},{8,9},{9,10},{10,1... | collective-permute-start | bytes 190472 | tf_op jit(solution)/shard_map/ppermute | solution.py:1124
  (339 other events, 4270.6 us)
where the time goes:
time: 950 us; the launch traced here: 938 us
  waiting for transfers between devices  313 us (33%)
  starting transfers between devices  157 us (17%)
  Pallas kernels  155 us (16%)
  other arithmetic  127 us (13%)
  matrix products  88.1 us (9%)
  local copies, waits for them, and re-layouts  82.2 us (9%)
  between operations  15.9 us (2%)
    ppermute x126, waiting for transfers between devices, swap(): return lax.ppermute(value, axis, [(i, i ^ mask) for i in range(count)])  313 us
    ppermute x126, starting transfers between devices, swap(): return lax.ppermute(value, axis, [(i, i ^ mask) for i in range(count)])  154 us
    dot_general x12, matrix products, times_back(): lax.dot_general(left_side, right_side, (((1,), (1,)), ((), ())), preferre...  34.6 us
    pallas_call x3, Pallas kernels, attend_backward(): pl.pallas_call(partial(attend_backward_kernel, causal), grid=(rows // til...  29.8 us
    dot_general x11, matrix products, times(): return jnp.dot(left_side, right_side, preferred_element_type=f32)  29.6 us
    unnamed x524, local copies, waits for them, and re-layouts  26.8 us
    pallas_call x3, Pallas kernels, attend_forward(): pl.pallas_call(partial(attend_forward_kernel, causal), grid=(rows // tile...  25.1 us
    pallas_call x5, Pallas kernels, write_lines(): pl.pallas_call(kernel, grid=(height // step,), in_specs=specs, out_specs=...  24.7 us
  transfers between devices with their start and end apart: 128, of which 59 were waited for; matrix products, arithmetic and copies ran while one was open for 23% of the time, Pallas kernels for 9%

commit v1 on v0

--- a/solution.py
+++ b/solution.py
@@ -157,12 +157,11 @@
     return jnp.stack([jnp.concatenate([r[k] for r in results]) for k in range(count)])
 
 
-def reduce_group(slots, wire, hold=f32):
+def reduce_group(even, odd, wire, hold=f32):
     count = lax.axis_size("grp")
-    sent = jnp.stack([slots[k] for k in range(count) if k & 1]).astype(wire)
-    came = swap(sent, "grp", 1)
-    held = {k: slots[k].astype(hold) + came[k // 2].astype(hold) for k in range(0, count, 2)}
-    half = slots[0].shape[0] // 2
+    came = swap(odd.astype(wire), "grp", 1)
+    held = {k: even[k // 2].astype(hold) + came[k // 2].astype(hold) for k in range(0, count, 2)}
+    half = even.shape[1] // 2
     results = []
     for low, order in zip((0, half), group_orders()):
         part = {k: v[low : low + half] for k, v in held.items()}
@@ -505,21 +504,29 @@
     return jnp.concatenate([rows, blank]).T
 
 
+def row_parts(rows):
+    step = rows // 4 if rows % 64 == 0 else rows
+    return [(low, low + step) for low in range(0, rows, step)]
+
+
 def loss_forward_kernel(last, rank_ref, here_ref, states_ref, table_ref, target_ref, out_ref):
     target = stand_up(jnp.broadcast_to(target_ref[0].astype(f32), (8, target_ref.shape[2])))
     target = target[:, 0:1].astype(jnp.int32)
 
-    def work(columns, short):
-        logits = times(states_ref[0], table_ref[:, :columns])
+    def part_of(columns, short, low, high):
+        logits = times(states_ref[0, low:high], table_ref[:, :columns])
         column = lax.broadcasted_iota(jnp.int32, logits.shape, 1)
         if short:
             logits = jnp.where(column < here_ref[0], logits, masked_score)
         highest = jnp.max(logits, axis=1, keepdims=True)
         total = jnp.sum(jnp.exp(logits - highest), axis=1, keepdims=True)
-        picked = jnp.sum(jnp.where(column == target, logits, 0.0), axis=1, keepdims=True)
-        lane = lax.broadcasted_iota(jnp.int32, (logits.shape[0], LANES), 1)
-        packed = jnp.where(lane == 0, highest, jnp.where(lane == 1, total, picked))
-        out_ref[0] = packed.T[:8]
+        picked = jnp.sum(jnp.where(column == target[low:high], logits, 0.0), axis=1, keepdims=True)
+        lane = lax.broadcasted_iota(jnp.int32, (high - low, LANES), 1)
+        return jnp.where(lane == 0, highest, jnp.where(lane == 1, total, picked))
+
+    def work(columns, short):
+        packed = [part_of(columns, short, low, high) for low, high in row_parts(states_ref.shape[1])]
+        out_ref[0] = jnp.concatenate(packed).T[:8]
 
     width = table_ref.shape[1]
 
@@ -578,26 +585,51 @@
 
 
 def loss_backward_kernel(
-    last, rank_ref, here_ref, states_ref, table_ref, target_ref, scale_ref, grad_ref, out_ref
+    last,
+    rank_ref,
+    here_ref,
+    states_ref,
+    table_ref,
+    target_ref,
+    scale_ref,
+    grad_ref,
+    kept_ref,
+    sent_ref,
 ):
     target = stand_up(jnp.broadcast_to(target_ref[0].astype(f32), (8, target_ref.shape[2])))
     target = target[:, 0:1].astype(jnp.int32)
     scale = stand_up(scale_ref[0])
 
-    def work(columns, short):
-        logits = times(states_ref[0], table_ref[:, :columns])
+    odd = pl.program_id(0) % 2
+
+    def part_of(columns, short, low, high):
+        logits = times(states_ref[0, low:high], table_ref[:, :columns])
         column = lax.broadcasted_iota(jnp.int32, logits.shape, 1)
-        soft = jnp.exp(logits - scale[:, 0:1])
-        grad = jnp.where(column == target, soft - 1.0, soft) * scale[:, 1:2]
+        soft = jnp.exp(logits - scale[low:high, 0:1])
+        grad = jnp.where(column == target[low:high], soft - 1.0, soft) * scale[low:high, 1:2]
         if short:
             grad = jnp.where(column < here_ref[0], grad, 0.0)
         grad = grad.astype(bf16)
-        grad_ref[0, :, :columns] = grad
+        grad_ref[0, low:high, :columns] = grad
         if columns < grad_ref.shape[2]:
-            grad_ref[0, :, columns:] = jnp.zeros(
-                (grad.shape[0], grad_ref.shape[2] - columns), bf16
+            grad_ref[0, low:high, columns:] = jnp.zeros(
+                (high - low, grad_ref.shape[2] - columns), bf16
             )
-        out_ref[0] = times_back(grad, table_ref[:, :columns])
+        return times_back(grad, table_ref[:, :columns])
+
+    def work(columns, short):
+        parts = [(0, states_ref.shape[1])]
+        grads = [part_of(columns, short, low, high) for low, high in parts]
+
+        @pl.when(odd == 0)
+        def _():
+            for (low, high), grad in zip(parts, grads):
+                kept_ref[0, low:high] = grad
+
+        @pl.when(odd == 1)
+        def _():
+            for (low, high), grad in zip(parts, grads):
+                sent_ref[0, low:high] = grad.astype(bf16)
 
     width = table_ref.shape[1]
 
@@ -626,12 +658,14 @@
             ],
             out_specs=[
                 pl.BlockSpec((1, tile, width), lambda i, rank, here: (i, 0, 0)),
-                pl.BlockSpec((1, tile, deep), lambda i, rank, here: (i, 0, 0)),
+                pl.BlockSpec((1, tile, deep), lambda i, rank, here: (i // 2, 0, 0)),
+                pl.BlockSpec((1, tile, deep), lambda i, rank, here: (i // 2, 0, 0)),
             ],
         ),
         out_shape=[
             jax.ShapeDtypeStruct((count, tile, width), bf16),
-            jax.ShapeDtypeStruct((count, tile, deep), f32),
+            jax.ShapeDtypeStruct((count // 2, tile, deep), f32),
+            jax.ShapeDtypeStruct((count // 2, tile, deep), bf16),
         ],
         name="loss_backward",
     )(rank.reshape(1), here.reshape(1), states, table, targets, scales)
@@ -803,8 +837,10 @@
     table = jnp.concatenate(reorder([piece[:chans] for piece in table_came], group_rank))
     vocab_first = seq_rank * vocab + group_rank * width
     vocab_here = jnp.clip(vocab - group_rank * width, 0, width)
-    ids_slots = jnp.stack([piece[chans:] for piece in table_came]).reshape(grp_size, -1)
-    ids_slots = ids_slots[:, : 4 * LEN].astype(jnp.int32).reshape(grp_size, 2, 2, LEN)
+    ids_rows = round_up(4 * LEN, width) // width
+    ids_slots = jnp.stack([piece[chans : chans + ids_rows] for piece in table_came])
+    ids_slots = ids_slots.reshape(grp_size, -1)[:, : 4 * LEN].astype(jnp.int32)
+    ids_slots = ids_slots.reshape(grp_size, 2, 2, LEN)
     ids_slots = ids_slots[:, 0] * 256 + ids_slots[:, 1]
 
     small = (7 + 7 + 11) * D + 2 * F
@@ -909,7 +945,7 @@
         mine = scatter_near(reorder(pieces, seq_rank), "seq", wire)
         return jnp.concatenate(reorder(gather_near(mine.astype(wire), "seq"), seq_rank))
 
-    token_emb = reduce_group(looked, bf16, bf16)
+    token_emb = reduce_group(looked[::2], looked[1::2], bf16, bf16)
     token_emb = share_rows(token_emb, bf16).astype(f32)
 
     def all_heads(value):
@@ -951,10 +987,10 @@
     row_weight = valid / token_total
     scales = jnp.stack([log_total, row_weight], axis=1)
     loss_sum = jnp.sum((log_total - stats[:, 2]) * valid)
-    grad_logits, grad_states_all = loss_backward(
+    grad_logits, states_kept, states_sent = loss_backward(
         all_states, table, target_rows, scales, vocab_here, group_rank, last
     )
-    grad_states = share_rows(reduce_group(grad_states_all, bf16), bf16).astype(f32)
+    grad_states = share_rows(reduce_group(states_kept, states_sent, bf16), bf16).astype(f32)
 
     table_main = lax.optimization_barrier(
         over_rows(all_states.reshape(-1, D), grad_logits.reshape(-1, width))

time: 950 us -> 944 us (level)
  local copies, waits for them, and re-layouts: 82.2 us -> 65.4 us
  waiting for transfers between devices: 313 us -> 327 us
    ppermute x126, waiting for transfers between devices: 313 us -> 327 us  [swap(): return lax.ppermute(value, axis, [(i, i ^ mask) for i in range(count)])]
    unnamed x524 -> x508, local copies, waits for them, and re-layouts: 26.8 us -> 20.9 us
  transfers between devices with their start and end apart: 128 -> 128, of which waited for: 59 -> 58; matrix products, arithmetic and copies ran while one was open for 23% -> 22% of each run, Pallas kernels for 9% -> 9%
where the time goes in v1:
time: 944 us; the launch traced here: 933 us
  waiting for transfers between devices  327 us (35%)
  Pallas kernels  156 us (17%)
  starting transfers between devices  152 us (16%)
  other arithmetic  126 us (13%)
  matrix products  89.5 us (9%)
  local copies, waits for them, and re-layouts  65.4 us (7%)
  between operations  16.1 us (2%)
    ppermute x126, waiting for transfers between devices, swap(): return lax.ppermute(value, axis, [(i, i ^ mask) for i in range(count)])  327 us
    ppermute x126, starting transfers between devices, swap(): return lax.ppermute(value, axis, [(i, i ^ mask) for i in range(count)])  146 us
    dot_general x12, matrix products, times_back(): lax.dot_general(left_side, right_side, (((1,), (1,)), ((), ())), preferre...  36 us
    pallas_call x3, Pallas kernels, attend_backward(): pl.pallas_call(partial(attend_backward_kernel, causal), grid=(rows // til...  29.8 us
    dot_general x11, matrix products, times(): return jnp.dot(left_side, right_side, preferred_element_type=f32)  29.5 us
    pallas_call x3, Pallas kernels, attend_forward(): pl.pallas_call(partial(attend_forward_kernel, causal), grid=(rows // tile...  25.1 us
    pallas_call x5, Pallas kernels, write_lines(): pl.pallas_call(kernel, grid=(height // step,), in_specs=specs, out_specs=...  24.7 us
    dot_general x2, matrix products, over_rows(): lax.dot_general(left_side, right_side, (((0,), (0,)), ((), ())), preferre...  24 us
  transfers between devices with their start and end apart: 128, of which 58 were waited for; matrix products, arithmetic and copies ran while one was open for 22% of the time, Pallas kernels for 9%

profile of v1, /device:TPU:0, one launch (start us, length us, event | category | flops | bytes accessed | tf_op | source)
XLA Modules:
  0.0 933.2 jit_solution(6770652442074513983)
XLA Ops:
  33.8 9.1 collective-permute-done.21
  45.0 9.6 %collective-permute-done.20 = bf16[832,128]{1,0:T(8,128)(2,1)S(1)} collective-permute-done((bf16[832,128]{1,0:T(8,128)(2,1)S(1)}, bf16[832,128]{1,0:T(8,128)(2,1)S(1)}, u32[]{:S(2)}, u32[]{:S(2)}) %collective-permute-start.20) | collective-permute-done | bytes 213024 | tf_op jit(solution)/shard_map/ppermute | solution.py:84
  77.6 13.8 %collective-permute-done.4 = bf16[80,1664]{1,0:T(8,128)(2,1)S(1)} collective-permute-done((bf16[80,1664]{1,0:T(8,128)(2,1)S(1)}, bf16[80,1664]{1,0:T(8,128)(2,1)S(1)}, u32[]{:S(2)}, u32[]{:S(2)}) %collective-permute-start.4) | collective-permute-done | bytes 266272 | tf_op jit(solution)/shard_map/ppermute | solution.py:84
  105.0 9.5 %fusion.9 = bf16[3584,512]{1,0:T(8,128)(2,1)S(1)} fusion(bf16[512,1664]{1,0:T(8,128)(2,1)} %select_dynamic-update-slice_fusion.8.table_ref, s32[3584]{0:T(1024)S(1)} %sub.190, pred[1664]{0:T(1024)(128)(4,1)S(1)} %iota_compare_fusion.3), kind=kOutput, calls=%fused_computation.8 | convolution fusion | flops 6120669184 | bytes 5389952 | tf_op jit(solution)/shard_map/dot_general | solution.py:67
  132.9 8.3 collective-permute-done.23
  154.6 10.6 %collective-permute-done.10 = bf16[2,224,512]{2,1,0:T(8,128)(2,1)S(1)} collective-permute-done((bf16[2,224,512]{2,1,0:T(8,128)(2,1)S(1)}, bf16[2,224,512]{2,1,0:T(8,128)(2,1)S(1)}, u32[]{:S(2)}, u32[]{:S(2)}) %collective-permute-start.10) | collective-permute-done | bytes 458784 | tf_op jit(solution)/shard_map/ppermute | solution.py:84
  166.6 8.3 collective-permute-done.32
  176.5 10.5 %collective-permute-done.34 = bf16[2,4,512,128]{3,2,1,0:T(8,128)(2,1)S(1)} collective-permute-done((bf16[2,4,512,128]{3,2,1,0:T(8,128)(2,1)S(1)}, bf16[2,4,512,128]{3,2,1,0:T(8,128)(2,1)S(1)}, u32[]{:S(2)}, u32[]{:S(2)}) %collective-permute-start.34) | collective-permute-done | bytes 1048608 | tf_op jit(solution)/shard_map/ppermute | solution.py:84
  192.3 9.7 %lay_out.2 = (bf16[512,1536]{1,0:T(8,128)(2,1)}, bf16[512,512]{1,0:T(8,128)(2,1)}, bf16[512,2048]{1,0:T(8,128)(2,1)}, bf16[2048,512]{1,0:T(8,128)(2,1)}, bf16[44...) custom-call(s32[1]{0:T(128)} %bitcast.8.rank_ref, bf16[4,4,416,128]{3,2,1,0:T(8,128)(2,1)} %copy-done.23, ...), custom_call_target="tpu_custom_call" | custom-call | tf_op jit(solution)/shard_map/lay_out/pallas_call | solution.py:253
  209.9 17.3 %attend_forward.4 = (bf16[1536,128]{1,0:T(8,128)(2,1)}, f32[2,1536]{1,0:T(2,128)}) custom-call(bf16[1536,128]{1,0:T(8,128)(2,1)} %get-tuple-element.194.query_ref, bf16[1536,128]{1,0:T(8,128)(2,1)} %slice.1635.key_ref, bf16[1536,128]{1,0:T(8,128)(2,1)} %get-tuple-element.193.value_ref, f32[1536,1]{1,0:T(8,128)} %fusion.49.bias_ref), custom_call_target="tpu_custom_call" | custom-call | tf_op jit(solution)/shard_map/attend_forward/pallas_call | solution.py:414
  238.2 8.0 collective-permute-done.44
  250.1 9.5 %multiply_convert_fusion.1 = (bf16[384,2048]{1,0:T(8,128)(2,1)S(1)}, f32[384,2048]{1,0:T(8,128)}, f32[384,2048]{1,0:T(8,128)}) fusion(f32[2048]{0:T(1024)S(1)} %get-tuple-element.365, bf16[384,512]{1,0:T(8,128)(2,1)S(1)} %add_convert_fusion.11.refs_0_, bf16[512,2048]{1,0:T(8,128)(2,1)S(1)} %copy-done.226), kind=kOutput, calls=%fused_computation.42 | convolution fusion | flops 857210880 | bytes 10362880 | tf_op jit(solution)/shard_map/dot_general | solution.py:63
  274.5 11.7 %lay_out.3 = (bf16[512,1536]{1,0:T(8,128)(2,1)}, bf16[512,512]{1,0:T(8,128)(2,1)}, bf16[512,512]{1,0:T(8,128)(2,1)}, bf16[512,1024]{1,0:T(8,128)(2,1)}, bf16[512...) custom-call(s32[1]{0:T(128)} %bitcast.8.rank_ref, ...), custom_call_target="tpu_custom_call" | custom-call | tf_op jit(solution)/shard_map/lay_out/pallas_call | solution.py:253
  304.0 9.0 collective-permute-done.38
  340.8 10.4 %multiply_convert_fusion = (bf16[448,2048]{1,0:T(8,128)(2,1)S(1)}, f32[448,2048]{1,0:T(8,128)}, f32[448,2048]{1,0:T(8,128)}) fusion(f32[2048]{0:T(1024)S(1)} %copy-done.196, bf16[448,512]{1,0:T(8,128)(2,1)S(1)} %add_convert_fusion.5.refs_8_, bf16[512,2048]{1,0:T(8,128)(2,1)S(1)} %copy-done.229), kind=kOutput, calls=%fused_computation.17 | convolution fusion | flops 1000079360 | bytes 11739136 | tf_op jit(solution)/shard_map/dot_general | solution.py:63
  364.1 14.5 %collective-permute-done.52 = bf16[1,224,512]{2,1,0:T(8,128)(2,1)S(1)} collective-permute-done((bf16[1,224,512]{2,1,0:T(8,128)(2,1)S(1)}, bf16[1,224,512]{2,1,0:T(8,128)(2,1)S(1)}, u32[]{:S(2)}, u32[]{:S(2)}) %collective-permute-start.52) | collective-permute-done | bytes 229408 | tf_op jit(solution)/shard_map/ppermute | solution.py:84
  380.5 8.9 collective-permute-done.53
  397.8 16.4 %loss_forward.1.refs_0_ = f32[8,8,448]{2,1,0:T(8,128)} custom-call(s32[1]{0:T(128)} %bitcast.rank_ref, s32[1]{0:T(128)} %bitcast.1.here_ref, bf16[8,448,512]{2,1,0:T(8,128)(2,1)} %fusion.87.states_ref, bf16[512,1664]{1,0:T(8,128)(2,1)} %select_dynamic-update-slice_fusion.8.table_ref, s32[8,1,448]{2,1,0:T(1,128)} %get-tuple-element.372.target_ref), custom_call_target="tpu_custom_call" | custom-call | tf_op jit(solution)/shard_map/loss_forward/pallas_call | solution.py:544
  448.4 21.2 %loss_backward.1 = (bf16[8,448,1664]{2,1,0:T(8,128)(2,1)}, f32[4,448,512]{2,1,0:T(8,128)}, bf16[4,448,512]{2,1,0:T(8,128)(2,1)}) custom-call(s32[1]{0:T(128)} %bitcast.rank_ref, s32[1]{0:T(128)} %bitcast.1.here_ref, bf16[8,448,512]{2,1,0:T(8,128)(2,1)} %fusion.87.states_ref, bf16[512,1664]{1,0:T(8,128)(2,1)} %select_dynamic-update-slice_fusion.8.table_ref, ...), custom_call_target="tpu_custom_call" | custom-call | tf_op jit(solution)/shard_map/loss_backward/pallas_call | solution.py:648
  508.2 13.2 %convolution_bitcast_fusion = f32[512,1664]{1,0:T(8,128)} fusion(bf16[8,448,512]{2,1,0:T(8,128)(2,1)} %fusion.87.states_ref, bf16[8,448,1664]{2,1,0:T(8,128)(2,1)} %get-tuple-element.72), kind=kOutput, calls=%fused_computation.35 | convolution fusion | flops 6106906624 | bytes 19005440 | tf_op jit(solution)/shard_map/dot_general | solution.py:73
  549.7 7.1 attend_backward.3
  644.8 19.3 %attend_backward.5 = (bf16[1536,128]{1,0:T(8,128)(2,1)}, bf16[1536,128]{1,0:T(8,128)(2,1)}, bf16[1536,128]{1,0:T(8,128)(2,1)}) custom-call(bf16[1536,128]{1,0:T(8,128)(2,1)} %pad_maximum_fusion.30.grad_ref, bf16[1536,128]{1,0:T(8,128)(2,1)} %get-tuple-element.194.query_ref, bf16[1536,128]{1,0:T(8,128)(2,1)} %slice.1635.key_ref, ...), custom_call_target="tpu_custom_call" | custom-call | tf_op jit(solution)/shard_map/attend_backward/pallas_call | solution.py:480
  690.8 7.3 constant_dynamic-slice_fusion.17
  703.4 7.8 own_blocks.1
  726.1 10.8 %fusion.20 = f32[512,1664]{1,0:T(8,128)S(1)} fusion(f32[512,1664]{1,0:T(8,128)} %convolution_bitcast_fusion, bf16[3584,512]{1,0:T(8,128)(2,1)} %bitcast.552, s32[3584]{0:T(1024)S(1)} %copy-done.175, pred[1664]{0:T(1024)(128)(4,1)S(1)} %copy-done.212), kind=kOutput, calls=%fused_computation.36 | convolution fusion | flops 6119686144 | bytes 10501760 | tf_op jit(solution)/shard_map/dot_general | solution.py:73
  751.3 7.8 collective-permute-done.119
  759.6 19.4 %collective-permute-done.117 = f32[64,1664]{1,0:T(8,128)S(1)} collective-permute-done((f32[64,1664]{1,0:T(8,128)S(1)}, f32[64,1664]{1,0:T(8,128)S(1)}, u32[]{:S(2)}, u32[]{:S(2)}) %collective-permute-start.117) | collective-permute-done | bytes 426016 | tf_op jit(solution)/shard_map/ppermute | solution.py:84
  788.1 9.5 %collective-permute-done.106 = f32[1,2,512,128]{3,2,1,0:T(8,128)S(1)} collective-permute-done((f32[1,2,512,128]{3,2,1,0:T(8,128)S(1)}, f32[1,2,512,128]{3,2,1,0:T(8,128)S(1)}, u32[]{:S(2)}, u32[]{:S(2)}) %collective-permute-start.106) | collective-permute-done | bytes 524320 | tf_op jit(solution)/shard_map/ppermute | solution.py:84
  805.0 20.2 %collective-permute-done.94 = f32[2,1,2,416,128]{4,3,2,1,0:T(8,128)S(1)} collective-permute-done((f32[2,1,2,416,128]{4,3,2,1,0:T(8,128)S(1)}, f32[2,1,2,416,128]{4,3,2,1,0:T(8,128)S(1)}, u32[]{:S(2)}, u32[]{:S(2)}) %collective-permute-start.94) | collective-permute-done | bytes 852000 | tf_op jit(solution)/shard_map/ppermute | solution.py:84
  828.7 13.1 %collective-permute-done.88 = f32[2,1,2,416,128]{4,3,2,1,0:T(8,128)S(1)} collective-permute-done((f32[2,1,2,416,128]{4,3,2,1,0:T(8,128)S(1)}, f32[2,1,2,416,128]{4,3,2,1,0:T(8,128)S(1)}, u32[]{:S(2)}, u32[]{:S(2)}) %collective-permute-start.88) | collective-permute-done | bytes 852000 | tf_op jit(solution)/shard_map/ppermute | solution.py:84
  848.5 7.7 collective-permute-done.95
  867.9 17.0 %collective-permute-done.98 = f32[832,128]{1,0:T(8,128)S(1)} collective-permute-done((f32[832,128]{1,0:T(8,128)S(1)}, f32[832,128]{1,0:T(8,128)S(1)}, u32[]{:S(2)}, u32[]{:S(2)}) %collective-permute-start.98) | collective-permute-done | bytes 426016 | tf_op jit(solution)/shard_map/ppermute | solution.py:84
  (1090 shorter events, 540.6 us)
Async XLA Ops:
  2.5 61.6 %collective-permute-start.30 = (bf16[1024,128]{1,0:T(8,128)(2,1)}, bf16[1024,128]{1,0:T(8,128)(2,1)}, u32[]{:S(2)}, u32[]{:S(2)}) collective-permute-start(bf16[1024,128]{1,0:T(8,128)(2,1)} %convert_bitcast_fusion), channel_id=1, source_target_pairs={{0,3},{1,2},{2,1},{3,0},{4,7},{5,6},{6,5},{7,4},{8,11},{9,10},{10,... | collective-permute-start | bytes 786440 | tf_op jit(solution)/shard_map/ppermute | solution.py:84
  7.5 58.4 %collective-permute-start.29 = (bf16[1024,128]{1,0:T(8,128)(2,1)}, bf16[1024,128]{1,0:T(8,128)(2,1)}, u32[]{:S(2)}, u32[]{:S(2)}) collective-permute-start(bf16[1024,128]{1,0:T(8,128)(2,1)} %convert_bitcast_fusion), channel_id=1, source_target_pairs={{0,2},{1,3},{2,0},{3,1},{4,6},{5,7},{6,4},{7,5},{8,10},{9,11},{10,... | collective-permute-start | bytes 786440 | tf_op jit(solution)/shard_map/ppermute | solution.py:84
  7.5 59.9 %collective-permute-start.28 = (bf16[1024,128]{1,0:T(8,128)(2,1)}, bf16[1024,128]{1,0:T(8,128)(2,1)}, u32[]{:S(2)}, u32[]{:S(2)}) collective-permute-start(bf16[1024,128]{1,0:T(8,128)(2,1)} %convert_bitcast_fusion), channel_id=1, source_target_pairs={{0,1},{1,0},{2,3},{3,2},{4,5},{5,4},{6,7},{7,6},{8,9},{9,8},{10,11... | collective-permute-start | bytes 786440 | tf_op jit(solution)/shard_map/ppermute | solution.py:84
  17.8 50.0 %collective-permute-start = (bf16[80,1664]{1,0:T(8,128)(2,1)}, bf16[80,1664]{1,0:T(8,128)(2,1)}, u32[]{:S(2)}, u32[]{:S(2)}) collective-permute-start(bf16[80,1664]{1,0:T(8,128)(2,1)} %get-tuple-element.201), channel_id=1, source_target_pairs={{0,4},{4,0},{8,12},{12,8},{16,20},{20,16},{24,28},{28,24},{1,5},{5... | collective-permute-start | bytes 798728 | tf_op jit(solution)/shard_map/ppermute | solution.py:84
  75.9 40.0 %collective-permute-start.42 = (bf16[384,512]{1,0:T(8,128)(2,1)}, bf16[384,512]{1,0:T(8,128)(2,1)}, u32[]{:S(2)}, u32[]{:S(2)}) collective-permute-start(bf16[384,512]{1,0:T(8,128)(2,1)} %pad.18), channel_id=1, source_target_pairs={{0,3},{1,2},{2,1},{3,0},{4,7},{5,6},{6,5},{7,4},{8,11},{9,10},{10,... | collective-permute-start | bytes 1179656 | tf_op jit(solution)/shard_map/ppermute | solution.py:84
  76.4 44.6 %collective-permute-start.41 = (bf16[384,512]{1,0:T(8,128)(2,1)}, bf16[384,512]{1,0:T(8,128)(2,1)}, u32[]{:S(2)}, u32[]{:S(2)}) collective-permute-start(bf16[384,512]{1,0:T(8,128)(2,1)} %pad.18), channel_id=1, source_target_pairs={{0,2},{1,3},{2,0},{3,1},{4,6},{5,7},{6,4},{7,5},{8,10},{9,11},{10,... | collective-permute-start | bytes 1179656 | tf_op jit(solution)/shard_map/ppermute | solution.py:84
  114.8 35.5 %collective-permute-start.7 = (bf16[4,448,512]{2,1,0:T(8,128)(2,1)S(1)}, bf16[4,448,512]{2,1,0:T(8,128)(2,1)S(1)}, u32[]{:S(2)}, u32[]{:S(2)}) collective-permute-start(bf16[4,448,512]{2,1,0:T(8,128)(2,1)S(1)} %get-tuple-element.181), channel_id=1, source_target_pairs={{0,4},{4,0},{8,12},{12,8},{16,20},{20,16},{24,28},{28,24},{1,5},{5... | collective-permute-start | bytes 5505032 | tf_op jit(solution)/shard_map/ppermute | solution.py:84
  132.3 42.6 %collective-permute-start.32 = (bf16[2,4,512,128]{3,2,1,0:T(8,128)(2,1)S(1)}, bf16[2,4,512,128]{3,2,1,0:T(8,128)(2,1)S(1)}, u32[]{:S(2)}, u32[]{:S(2)}) collective-permute-start(bf16[2,4,512,128]{3,2,1,0:T(8,128)(2,1)S(1)} %pad_maximum_fusion.5), channel_id=1, source_target_pairs={{0,16},{4,20},{8,24},{12,28},{16,0},{20,4},{24,8},{28,12},{1,17},{... | collective-permute-start | bytes 3145736 | tf_op jit(solution)/shard_map/ppermute | solution.py:84
  142.5 47.3 %collective-permute-start.26 = (bf16[4,4,416,128]{3,2,1,0:T(8,128)(2,1)S(1)}, bf16[4,4,416,128]{3,2,1,0:T(8,128)(2,1)S(1)}, u32[]{:S(2)}, u32[]{:S(2)}) collective-permute-start(bf16[4,4,416,128]{3,2,1,0:T(8,128)(2,1)S(1)} %pad_maximum_fusion.3.own_a), channel_id=1, source_target_pairs={{0,4},{4,0},{8,12},{12,8},{16,20},{20,16},{24,28},{28,24},{1,5},{5... | collective-permute-start | bytes 5111816 | tf_op jit(solution)/shard_map/ppermute | solution.py:84
  150.3 40.5 %collective-permute-start.27 = (bf16[4,4,416,128]{3,2,1,0:T(8,128)(2,1)S(1)}, bf16[4,4,416,128]{3,2,1,0:T(8,128)(2,1)S(1)}, u32[]{:S(2)}, u32[]{:S(2)}) collective-permute-start(bf16[4,4,416,128]{3,2,1,0:T(8,128)(2,1)S(1)} %pad_maximum_fusion.4.own_b), channel_id=1, source_target_pairs={{0,4},{4,0},{8,12},{12,8},{16,20},{20,16},{24,28},{28,24},{1,5},{5... | collective-permute-start | bytes 5111816 | tf_op jit(solution)/shard_map/ppermute | solution.py:84
  152.8 34.2 %collective-permute-start.34 = (bf16[2,4,512,128]{3,2,1,0:T(8,128)(2,1)S(1)}, bf16[2,4,512,128]{3,2,1,0:T(8,128)(2,1)S(1)}, u32[]{:S(2)}, u32[]{:S(2)}) collective-permute-start(bf16[2,4,512,128]{3,2,1,0:T(8,128)(2,1)S(1)} %pad_maximum_fusion.6), channel_id=1, source_target_pairs={{0,8},{4,12},{8,0},{12,4},{16,24},{20,28},{24,16},{28,20},{1,9},{5... | collective-permute-start | bytes 3145736 | tf_op jit(solution)/shard_map/ppermute | solution.py:84
  176.5 98.0 %collective-permute-start.35 = (bf16[4,4,512,128]{3,2,1,0:T(8,128)(2,1)}, bf16[4,4,512,128]{3,2,1,0:T(8,128)(2,1)}, u32[]{:S(2)}, u32[]{:S(2)}) collective-permute-start(bf16[4,4,512,128]{3,2,1,0:T(8,128)(2,1)} %pad_maximum_fusion.1.own_a), channel_id=1, source_target_pairs={{0,4},{4,0},{8,12},{12,8},{16,20},{20,16},{24,28},{28,24},{1,5},{5... | collective-permute-start | bytes 6291464 | tf_op jit(solution)/shard_map/ppermute | solution.py:84
  188.6 85.9 %collective-permute-start.36 = (bf16[4,4,512,128]{3,2,1,0:T(8,128)(2,1)}, bf16[4,4,512,128]{3,2,1,0:T(8,128)(2,1)}, u32[]{:S(2)}, u32[]{:S(2)}) collective-permute-start(bf16[4,4,512,128]{3,2,1,0:T(8,128)(2,1)} %pad_maximum_fusion.2.own_b), channel_id=1, source_target_pairs={{0,4},{4,0},{8,12},{12,8},{16,20},{20,16},{24,28},{28,24},{1,5},{5... | collective-permute-start | bytes 6291464 | tf_op jit(solution)/shard_map/ppermute | solution.py:84
  188.6 43.3 %collective-permute-start.11 = (bf16[1,224,512]{2,1,0:T(8,128)(2,1)}, bf16[1,224,512]{2,1,0:T(8,128)(2,1)S(1)}, u32[]{:S(2)}, u32[]{:S(2)}) collective-permute-start(bf16[1,224,512]{2,1,0:T(8,128)(2,1)} %get-tuple-element.306), channel_id=1, source_target_pairs={{0,16},{4,20},{8,24},{12,28},{16,0},{20,4},{24,8},{28,12},{1,17},{... | collective-permute-start | bytes 688136 | tf_op jit(solution)/shard_map/ppermute | solution.py:84
  189.9 44.5 %collective-permute-start.9 = (bf16[1,224,512]{2,1,0:T(8,128)(2,1)}, bf16[1,224,512]{2,1,0:T(8,128)(2,1)}, u32[]{:S(2)}, u32[]{:S(2)}) collective-permute-start(bf16[1,224,512]{2,1,0:T(8,128)(2,1)} %slice_add_fusion.15), channel_id=1, source_target_pairs={{0,8},{4,12},{8,0},{12,4},{16,24},{20,28},{24,16},{28,20},{1,9},{5... | collective-permute-start | bytes 688136 | tf_op jit(solution)/shard_map/ppermute | solution.py:84
  564.4 30.7 %collective-permute-start.82 = (bf16[384,256]{1,0:T(8,128)(2,1)}, bf16[384,256]{1,0:T(8,128)(2,1)}, u32[]{:S(2)}, u32[]{:S(2)}) collective-permute-start(bf16[384,256]{1,0:T(8,128)(2,1)} %get-tuple-element.245), channel_id=1, source_target_pairs={{0,2},{1,3},{2,0},{3,1},{4,6},{5,7},{6,4},{7,5},{8,10},{9,11},{10,... | collective-permute-start | bytes 589832 | tf_op jit(solution)/shard_map/ppermute | solution.py:84
  564.9 30.3 %collective-permute-start.81 = (bf16[384,256]{1,0:T(8,128)(2,1)}, bf16[384,256]{1,0:T(8,128)(2,1)}, u32[]{:S(2)}, u32[]{:S(2)}) collective-permute-start(bf16[384,256]{1,0:T(8,128)(2,1)} %get-tuple-element.246), channel_id=1, source_target_pairs={{0,3},{1,2},{2,1},{3,0},{4,7},{5,6},{6,5},{7,4},{8,11},{9,10},{10,... | collective-permute-start | bytes 589832 | tf_op jit(solution)/shard_map/ppermute | solution.py:84
  590.9 87.1 %collective-permute-start.79 = (bf16[448,384]{1,0:T(8,128)(2,1)}, bf16[448,384]{1,0:T(8,128)(2,1)}, u32[]{:S(2)}, u32[]{:S(2)}) collective-permute-start(bf16[448,384]{1,0:T(8,128)(2,1)} %constant_dynamic-update-slice_fusion), channel_id=1, source_target_pairs={{0,2},{1,3},{2,0},{3,1},{4,6},{5,7},{6,4},{7,5},{8,10},{9,11},{10,... | collective-permute-start | bytes 1032200 | tf_op jit(solution)/shard_map/ppermute | solution.py:84
  590.9 87.2 %collective-permute-start.78 = (bf16[448,384]{1,0:T(8,128)(2,1)}, bf16[448,384]{1,0:T(8,128)(2,1)}, u32[]{:S(2)}, u32[]{:S(2)}) collective-permute-start(bf16[448,384]{1,0:T(8,128)(2,1)} %constant_dynamic-update-slice_fusion), channel_id=1, source_target_pairs={{0,3},{1,2},{2,1},{3,0},{4,7},{5,6},{6,5},{7,4},{8,11},{9,10},{10,... | collective-permute-start | bytes 1032200 | tf_op jit(solution)/shard_map/ppermute | solution.py:84
  639.6 38.6 %collective-permute-start.80 = (bf16[448,384]{1,0:T(8,128)(2,1)}, bf16[448,384]{1,0:T(8,128)(2,1)}, u32[]{:S(2)}, u32[]{:S(2)}) collective-permute-start(bf16[448,384]{1,0:T(8,128)(2,1)} %constant_dynamic-update-slice_fusion), channel_id=1, source_target_pairs={{0,1},{1,0},{2,3},{3,2},{4,5},{5,4},{6,7},{7,6},{8,9},{9,8},{10,11... | collective-permute-start | bytes 1032200 | tf_op jit(solution)/shard_map/ppermute | solution.py:84
  640.3 73.7 %collective-permute-start.101 = (f32[1024,128]{1,0:T(8,128)}, f32[1024,128]{1,0:T(8,128)}, u32[]{:S(2)}, u32[]{:S(2)}) collective-permute-start(f32[1024,128]{1,0:T(8,128)} %get-tuple-element.206), channel_id=1, source_target_pairs={{0,2},{1,3},{2,0},{3,1},{4,6},{5,7},{6,4},{7,5},{8,10},{9,11},{10,... | collective-permute-start | bytes 1572872 | tf_op jit(solution)/shard_map/ppermute | solution.py:84
  642.1 71.9 %collective-permute-start.102 = (f32[1024,128]{1,0:T(8,128)}, f32[1024,128]{1,0:T(8,128)}, u32[]{:S(2)}, u32[]{:S(2)}) collective-permute-start(f32[1024,128]{1,0:T(8,128)} %get-tuple-element.205), channel_id=1, source_target_pairs={{0,3},{1,2},{2,1},{3,0},{4,7},{5,6},{6,5},{7,4},{8,11},{9,10},{10,... | collective-permute-start | bytes 1572872 | tf_op jit(solution)/shard_map/ppermute | solution.py:84
  678.1 36.0 %collective-permute-start.100 = (f32[1024,128]{1,0:T(8,128)}, f32[1024,128]{1,0:T(8,128)S(1)}, u32[]{:S(2)}, u32[]{:S(2)}) collective-permute-start(f32[1024,128]{1,0:T(8,128)} %get-tuple-element.204), channel_id=1, source_target_pairs={{0,1},{1,0},{2,3},{3,2},{4,5},{5,4},{6,7},{7,6},{8,9},{9,8},{10,11... | collective-permute-start | bytes 1572872 | tf_op jit(solution)/shard_map/ppermute | solution.py:84
  740.3 38.7 %collective-permute-start.117 = (f32[64,1664]{1,0:T(8,128)S(1)}, f32[64,1664]{1,0:T(8,128)S(1)}, u32[]{:S(2)}, u32[]{:S(2)}) collective-permute-start(f32[64,1664]{1,0:T(8,128)S(1)} %get-tuple-element.186), channel_id=1, source_target_pairs={{0,16},{4,20},{8,24},{12,28},{16,0},{20,4},{24,8},{28,12},{1,17},{... | collective-permute-start | bytes 1277960 | tf_op jit(solution)/shard_map/ppermute | solution.py:84
  741.0 38.1 %collective-permute-start.114 = (f32[64,1664]{1,0:T(8,128)S(1)}, f32[64,1664]{1,0:T(8,128)S(1)}, u32[]{:S(2)}, u32[]{:S(2)}) collective-permute-start(f32[64,1664]{1,0:T(8,128)S(1)} %get-tuple-element.188), channel_id=1, source_target_pairs={{0,28},{4,24},{8,20},{12,16},{16,12},{20,8},{24,4},{28,0},{1,29},{... | collective-permute-start | bytes 1277960 | tf_op jit(solution)/shard_map/ppermute | solution.py:84
  748.8 30.3 %collective-permute-start.115 = (f32[64,1664]{1,0:T(8,128)S(1)}, f32[64,1664]{1,0:T(8,128)S(1)}, u32[]{:S(2)}, u32[]{:S(2)}) collective-permute-start(f32[64,1664]{1,0:T(8,128)S(1)} %get-tuple-element.182), channel_id=1, source_target_pairs={{0,24},{4,28},{8,16},{12,20},{16,8},{20,12},{24,0},{28,4},{1,25},{... | collective-permute-start | bytes 1277960 | tf_op jit(solution)/shard_map/ppermute | solution.py:84
  759.1 40.0 %collective-permute-start.93 = (f32[2,2,2,832,128]{4,3,2,1,0:T(8,128)}, f32[2,2,2,832,128]{4,3,2,1,0:T(8,128)S(1)}, u32[]{:S(2)}, u32[]{:S(2)}) collective-permute-start(f32[2,2,2,832,128]{4,3,2,1,0:T(8,128)} %bitcast.126), channel_id=1, source_target_pairs={{0,4},{4,0},{8,12},{12,8},{16,20},{20,16},{24,28},{28,24},{1,5},{5... | collective-permute-start | bytes 10223624 | tf_op jit(solution)/shard_map/ppermute | solution.py:84
  759.1 44.3 %collective-permute-start.87 = (f32[2,2,2,832,128]{4,3,2,1,0:T(8,128)}, f32[2,2,2,832,128]{4,3,2,1,0:T(8,128)S(1)}, u32[]{:S(2)}, u32[]{:S(2)}) collective-permute-start(f32[2,2,2,832,128]{4,3,2,1,0:T(8,128)} %bitcast.119), channel_id=1, source_target_pairs={{0,4},{4,0},{8,12},{12,8},{16,20},{20,16},{24,28},{28,24},{1,5},{5... | collective-permute-start | bytes 10223624 | tf_op jit(solution)/shard_map/ppermute | solution.py:84
  797.7 68.7 %collective-permute-start.107 = (f32[1,1,512,128]{3,2,1,0:T(8,128)S(1)}, f32[1,1,512,128]{3,2,1,0:T(8,128)S(1)}, u32[]{:S(2)}, u32[]{:S(2)}) collective-permute-start(f32[1,1,512,128]{3,2,1,0:T(8,128)S(1)} %constant_dynamic-slice_fusion.7), channel_id=1, source_target_pairs={{0,8},{4,12},{8,0},{12,4},{16,24},{20,28},{24,16},{28,20},{1,9},{5... | collective-permute-start | bytes 786440 | tf_op jit(solution)/shard_map/ppermute | solution.py:84
  801.1 65.3 %collective-permute-start.105 = (f32[1,1,512,128]{3,2,1,0:T(8,128)S(1)}, f32[1,1,512,128]{3,2,1,0:T(8,128)S(1)}, u32[]{:S(2)}, u32[]{:S(2)}) collective-permute-start(f32[1,1,512,128]{3,2,1,0:T(8,128)S(1)} %constant_dynamic-slice_fusion.9), channel_id=1, source_target_pairs={{0,16},{4,20},{8,24},{12,28},{16,0},{20,4},{24,8},{28,12},{1,17},{... | collective-permute-start | bytes 786440 | tf_op jit(solution)/shard_map/ppermute | solution.py:84
  804.2 37.6 %collective-permute-start.88 = (f32[2,1,2,416,128]{4,3,2,1,0:T(8,128)S(1)}, f32[2,1,2,416,128]{4,3,2,1,0:T(8,128)S(1)}, u32[]{:S(2)}, u32[]{:S(2)}) collective-permute-start(f32[2,1,2,416,128]{4,3,2,1,0:T(8,128)S(1)} %constant_dynamic-slice_fusion.22), channel_id=1, source_target_pairs={{0,8},{4,12},{8,0},{12,4},{16,24},{20,28},{24,16},{28,20},{1,9},{5... | collective-permute-start | bytes 2555912 | tf_op jit(solution)/shard_map/ppermute | solution.py:84
  894.1 35.1 %collective-permute-start.127 = (f32[15872]{0:T(1024)S(1)}, f32[15872]{0:T(1024)S(1)}, u32[]{:S(2)}, u32[]{:S(2)}) collective-permute-start(f32[15872]{0:T(1024)S(1)} %slice_bitcast_fusion.48), channel_id=1, source_target_pairs={{0,1},{1,2},{2,3},{3,4},{4,5},{5,6},{6,7},{7,8},{8,9},{9,10},{10,1... | collective-permute-start | bytes 190472 | tf_op jit(solution)/shard_map/ppermute | solution.py:1160
  (331 other events, 4531.4 us)
